TPU v7x, 512 devices: a whole 4x4x16 slice. The times are simulated.
512 devices in a mesh: line: 8 (over y_hi, x), bus: 32 (over y_lo, z), scen: 2 (over core).
Axes of the slice: x: 4, y: 4 (y_hi: 2, y_lo: 2; y = y_hi * 2 + y_lo), z: 16, core: 2. Of those that a mesh axis runs over, the one named last changes fastest.
Arguments:
- ptdf: bfloat16 [8192, 49152], P('line', 'bus'), may hold values from -0.0546875 to 0.0546875
- injections: bfloat16 [49152, 512], P('bus', 'scen'), may hold values from -6 to 6
- lodf: bfloat16 [8192, 2048], P(('line', 'bus')), may hold values from -3 to 3
- ratings: float32 [8192], P(('line', 'bus')), may hold values from 0.5 to 2
- outages: int32 [2048], replicated, may hold values from 0 to 8191, as said below
Outputs:
- overload: float32 [8192, 2048], P(('line', 'bus'))
Inputs may be any that keep to these rules, and one draw needn't show every extreme that they name: `outages`: 2048 distinct line indices.
All inputs are finite; a program needn't handle non-finite values.
Results may differ from a plain program's by a relative error of at most 0.0003.
Values sent between devices are 32-bit elements; how exact they have to be, the bound alone decides.
No kernel may reach another device: no remote copies, remote signals or barrier semaphores. Data moves between devices by JAX's collectives and lax.ppermute only.
A program may use at most 64 MiB of HBM per device.

v0:
```python
import jax
import jax.numpy as jnp
from jax import lax
from jax.sharding import PartitionSpec as P

softness = 0.2


def base_flow_term(base_rows, lodf_rows, outage_flow):
    return (
        base_rows[:, None, :] + lodf_rows.astype(jnp.float32)[:, :, None] * outage_flow[None, :, :]
    )


def overload_sum(base_flow, outage_flow, lodf, ratings):
    lines_here = base_flow.shape[0]
    groups = lines_here // 4

    def line_block(pieces):
        base_rows, lodf_rows, rating_rows = pieces
        post_flow = base_flow_term(base_rows, lodf_rows, outage_flow)
        margin = (jnp.abs(post_flow) - rating_rows[:, None, None]) / (
            softness * rating_rows[:, None, None]
        )
        return jnp.sum(jax.nn.sigmoid(margin), axis=2)

    summed = lax.map(
        line_block,
        (base_flow.reshape(groups, 4, -1), lodf.reshape(groups, 4, -1), ratings.reshape(groups, 4)),
    )
    return summed.reshape(lines_here, -1)


def select_rows(flows, outages, first):
    count = flows.shape[0]
    offset = outages - first
    inside = (offset >= 0) & (offset < count)
    picked = jnp.take(flows, jnp.clip(offset, 0, count - 1), axis=0)
    return jnp.where(inside[:, None], picked, 0.0)


def shards(ptdf, injections, lodf, ratings, outages):
    own_rows = lodf.shape[0]
    base_flow = lax.psum_scatter(
        jnp.dot(ptdf, injections, preferred_element_type=jnp.float32),
        "bus",
        scatter_dimension=0,
        tiled=True,
    )
    first_own = (lax.axis_index("line") * lax.axis_size("bus") + lax.axis_index("bus")) * own_rows
    outage_flow = lax.psum(select_rows(base_flow, outages, first_own), ("line", "bus"))
    local_sum = overload_sum(base_flow, outage_flow, lodf, ratings)
    total = lax.psum(local_sum, "scen")
    return total / (injections.shape[1] * lax.axis_size("scen"))


def solution(mesh):
    return jax.shard_map(
        shards,
        mesh=mesh,
        in_specs=(
            P("line", "bus"),
            P("bus", "scen"),
            P(("line", "bus"), None),
            P(("line", "bus")),
            P(),
        ),
        out_specs=P(("line", "bus"), None),
        check_vma=False,
    )
```

profile of v0, /device:TPU:1, one launch (start us, length us, event | category | flops | bytes accessed | tf_op | source)
XLA Modules:
  0.0 666.5 jit_solution(12721925452298086936)
XLA Ops:
  6.5 1.9 copy-done
  8.4 3.1 fusion.4
  11.5 0.0 all-reduce.3.cloned.1.call-start
  11.6 118.5 %reduce-scatter.2.cloned.1.call-done = f32[32,256]{1,0:T(8,128)} async-done(((f32[1024,256]{1,0:T(8,128)}), f32[32,256]{1,0:T(8,128)}) %reduce-scatter.2.cloned.1.call-update) | async-done | bytes 32784 | tf_op jit(solution)/shard_map/reduce_scatter | solution.py:44
  130.1 9.3 %gather_fusion = f32[2048,256]{1,0:T(8,128)} fusion(f32[32,256]{1,0:T(8,128)} %reduce-scatter.2.cloned.1.call-done, s32[2048]{0:T(1024)S(1)} %fusion.2), kind=kCustom, calls=%fused_computation | custom fusion | bytes 4202496 | tf_op jit(solution)/shard_map/jit(_take)/gather | solution.py:38
  139.4 4.3 select_select_fusion
  143.8 0.0 all-reduce.3.cloned.1.call-update
  143.8 0.0 all-reduce.5.cloned.1.call-start
  143.9 0.1 reshape.38
  143.9 0.1 reshape.39
  144.0 420.5 %all-reduce.3.cloned.1.call-done = f32[2048,256]{1,0:T(8,128)} async-done(((f32[2048,256]{1,0:T(8,128)}), f32[2048,256]{1,0:T(8,128)}) %all-reduce.3.cloned.1.call-update) | async-done | bytes 2097168 | tf_op jit(solution)/shard_map/psum | solution.py:51
  564.5 46.5 %while.10 = (s32[]{:T(128)}, f32[8,4,2048]{2,1,0:T(4,128)}, f32[8,4,256]{2,1,0:T(4,128)S(1)}, bf16[8,4,2048]{2,1,0:T(4,128)(2,1)S(1)}, f32[2048,256]{1,0:T(8,128)}, /*index=5*/f32[8,4]{1,0:T(8,128)S(1)}, s32[]{:T(128)}) while((s32[]{:T(128)}, f32[8,4,2048]{2,1,0:T(4,128)}, f32[8,4,256]{2,1,0:T(4,128)S(1)}, bf16[8,4,2048]{2,1,0:T(4,128)(2,1)S(1)}, ...), condition=%wide.region_4.5_spmd, body=%wide.region_2.4_spmd.sunk | while | flops 18874372 | bytes 2290345 | solution.py:27
  564.5 5.1 fusion.8
  569.7 0.6 bitcast_dynamic-update-slice_fusion.2
  570.4 5.1 fusion.8
  575.5 0.6 bitcast_dynamic-update-slice_fusion.2
  576.2 5.1 fusion.8
  581.3 0.6 bitcast_dynamic-update-slice_fusion.2
  582.0 5.1 fusion.8
  587.1 0.6 bitcast_dynamic-update-slice_fusion.2
  587.8 5.1 fusion.8
  592.9 0.6 bitcast_dynamic-update-slice_fusion.2
  593.6 5.1 fusion.8
  598.7 0.6 bitcast_dynamic-update-slice_fusion.2
  599.4 5.1 fusion.8
  604.5 0.6 bitcast_dynamic-update-slice_fusion.2
  605.2 5.1 fusion.8
  610.4 0.6 bitcast_dynamic-update-slice_fusion.2
  611.0 1.7 reshape.40
  612.7 0.0 all-reduce.5.cloned.1.call-update
  612.7 45.5 %all-reduce.5.cloned.1.call-done = f32[32,2048]{1,0:T(8,128)} async-done(((f32[32,2048]{1,0:T(8,128)}), f32[32,2048]{1,0:T(8,128)}) %all-reduce.5.cloned.1.call-update) | async-done | bytes 262160 | tf_op jit(solution)/shard_map/psum | solution.py:53
  658.3 1.7 broadcast_multiply_fusion.1
  (39 shorter events, 0.3 us)
Async XLA Ops:
  6.5 1.9 copy-start
  6.5 5.1 copy-start.3
  6.5 123.6 %reduce-scatter.2.cloned.1.call-start = ((), (), s32[]{:S(2)}) async-start(), calls=%async_computation.1 | async-start | bytes 1081344 | tf_op jit(solution)/shard_map/reduce_scatter | solution.py:44
  11.5 553.0 %all-reduce.3.cloned.1.call-start = ((), (), s32[]{:S(2)}) async-start(), calls=%async_computation.2 | async-start | bytes 4194304 | tf_op jit(solution)/shard_map/psum | solution.py:51
  139.4 4.4 copy-start.2
  139.4 4.5 copy-start.4
  139.4 4.6 copy-start.1
  143.8 514.5 %all-reduce.5.cloned.1.call-start = ((), (), s32[]{:S(2)}) async-start(), calls=%async_computation.3 | async-start | bytes 524288 | tf_op jit(solution)/shard_map/psum | solution.py:53
Sparse Core Ops, SparseCore 0:
  11.7 118.4 reduce-scatter.1
  143.9 420.5 all-reduce.2
  612.9 45.3 all-reduce.4
where the time goes:
time: 667 us; the launch traced here: 666 us
  waiting for transfers between devices  585 us (88%)
  other arithmetic  47.3 us (7%)
  local copies, waits for them, and re-layouts  18.2 us (3%)
  between operations  13.2 us (2%)
    psum x1, waiting for transfers between devices, shards(): lax.psum(select_rows(base_flow, outages, first_own), ('line', 'bus'))  420 us
    reduce_scatter x1, waiting for transfers between devices, shards(): lax.psum_scatter(jnp.dot(ptdf, injections, preferred_element_type=jnp.flo...  118 us
    psum x1, waiting for transfers between devices, shards(): total = lax.psum(local_sum, 'scen')  45.5 us
    reduce_sum x8, other arithmetic, line_block(): return jnp.sum(jax.nn.sigmoid(margin), axis=2)  41.2 us
  transfers between devices with their start and end apart: 3, of which 3 were waited for; matrix products, arithmetic and copies ran while one was open for 0% of the time, Pallas kernels for 0%

commit v1 on v0

v1 whole, which is shorter than its diff:
```python
import jax
import jax.numpy as jnp
from jax import lax
from jax.experimental import pallas as pl
from jax.experimental.pallas import tpu as pltpu
from jax.sharding import Mesh, PartitionSpec as P

softness = 0.2
PLANE = ("line", "yl")
EXACT = lax.Precision.HIGHEST


def overload_kernel(where_ref, flow_ref, base_ref, lodf_ref, gain_ref, out_ref, spread, rows, turned, scaled):
    lines, scens = base_ref.shape[1], base_ref.shape[0]
    tile = out_ref.shape[1]
    step = pl.program_id(0)

    @pl.when(step == 0)
    def _():
        for line in range(lines):
            spread[line] = jnp.broadcast_to(base_ref[:, line : line + 1], (scens, 128))

    def fetch(group, carry):
        for offset in range(8):
            slot = group * 8 + offset
            rows[pl.ds(slot, 1), :] = flow_ref[pl.ds(where_ref[step * tile + slot], 1), :]
        return carry

    lax.fori_loop(0, tile // 8, fetch, 0)
    for part in range(tile // 128):
        turned[:, part * 128 : part * 128 + 128] = rows[part * 128 : part * 128 + 128, :].T
    scaled[...] = lodf_ref[...].astype(jnp.float32) * gain_ref[...]

    def pair(index, carry):
        first = index * 2
        factors = []
        for j in range(2):
            row = scaled[pl.ds(first + j, 1), :]
            factors.append([jnp.broadcast_to(row[:, k : k + 128], (8, 128)) for k in range(0, tile, 128)])
        sums = [[jnp.zeros((8, 128), jnp.float32) for _ in range(0, tile, 128)] for j in range(2)]
        for s in range(0, scens, 8):
            for part in range(tile // 128):
                flow = turned[s : s + 8, part * 128 : part * 128 + 128]
                for j in range(2):
                    level = spread[first + j, s : s + 8, :] + factors[j][part] * flow
                    sums[j][part] = sums[j][part] + jnp.tanh(jnp.abs(level) - 0.5 / softness)
        for j in range(2):
            out_ref[pl.ds(first + j, 1), :] = jnp.concatenate(
                [jnp.sum(total, axis=0, keepdims=True) for total in sums[j]], axis=1
            )
        return carry

    lax.fori_loop(0, lines // 2, pair, 0)


def overload_sums(where, flow, base, lodf, gain):
    lines, outages = lodf.shape
    scens = base.shape[1]
    tile = min(256, outages)
    return pl.pallas_call(
        overload_kernel,
        out_shape=jax.ShapeDtypeStruct((lines, outages), jnp.float32),
        grid_spec=pltpu.PrefetchScalarGridSpec(
            num_scalar_prefetch=1,
            grid=(outages // tile,),
            in_specs=[
                pl.BlockSpec((outages, scens), lambda i, w: (0, 0), pipeline_mode=pl.Buffered(1)),
                pl.BlockSpec((scens, lines), lambda i, w: (0, 0), pipeline_mode=pl.Buffered(1)),
                pl.BlockSpec((lines, tile), lambda i, w: (0, i)),
                pl.BlockSpec((lines, 1), lambda i, w: (0, 0), pipeline_mode=pl.Buffered(1)),
            ],
            out_specs=pl.BlockSpec((lines, tile), lambda i, w: (0, i)),
            scratch_shapes=[
                pltpu.VMEM((lines, scens, 128), jnp.float32),
                pltpu.VMEM((tile, scens), jnp.float32),
                pltpu.VMEM((scens, tile), jnp.float32),
                pltpu.VMEM((lines, tile), jnp.float32),
            ],
        ),
        compiler_params=pltpu.CompilerParams(vmem_limit_bytes=24 << 20),
        cost_estimate=pl.CostEstimate(
            flops=5 * lines * outages * scens,
            transcendentals=lines * outages * scens,
            bytes_accessed=4 * outages * scens + 6 * lines * outages,
        ),
    )(where, flow, (base * gain).T, lodf, gain)


def exchange(values, axes):
    return lax.all_to_all(values, axes, 0, 0, tiled=True)


def gather_all(rows, axes, members):
    return exchange(jnp.tile(rows, (members, 1)), axes)


def shards(ptdf, injections, lodf, ratings, outages):
    own, count = lodf.shape
    scens = injections.shape[1]
    n_z, n_plane, n_yl = lax.axis_size("z"), lax.axis_size("line") * lax.axis_size("yl"), lax.axis_size("yl")
    column = own * n_z
    share = -(-column // n_plane)
    depth = count // n_plane
    here = lax.axis_index("line") * n_yl + lax.axis_index("yl")

    partial = jnp.dot(ptdf, injections, preferred_element_type=jnp.float32)
    yl = lax.axis_index("yl")
    sent = lax.dynamic_slice_in_dim(partial, (1 - yl) * column, column)
    kept = lax.dynamic_slice_in_dim(partial, yl * column, column)
    flows = kept + lax.ppermute(sent, "yl", [(0, 1), (1, 0)])

    rank = jnp.sum((outages[None, :] < outages[:, None]).astype(jnp.int32), axis=1)
    where = (rank % n_plane) * depth + rank // n_plane
    starts = jnp.sum(
        (outages[None, :] < (column * jnp.arange(n_plane + 1))[:, None]).astype(jnp.int32), axis=1
    )
    lines = here * column + jnp.arange(column)
    before = jnp.sum((outages[None, :] < lines[:, None]).astype(jnp.int32), axis=1)
    through = jnp.sum((outages[None, :] <= lines[:, None]).astype(jnp.int32), axis=1)
    start = jnp.sum((outages < here * column).astype(jnp.int32))
    slot = jnp.where(through > before, (before % n_plane) * share + (before - start) // n_plane, -1)
    deal = (slot[None, :] == jnp.arange(n_plane * share)[:, None]).astype(jnp.float32)

    dealt = exchange(jnp.dot(deal, flows, precision=EXACT), PLANE)
    turn = lax.rem(here - starts[:-1] + count * n_plane, n_plane)[:, None] + n_plane * jnp.arange(share)[None, :]
    place = starts[:-1][:, None] + turn
    place = jnp.where(place < starts[1:][:, None], place // n_plane, -1).reshape(-1)
    collect = (place[None, :] == jnp.arange(depth)[:, None]).astype(jnp.float32)
    collected = jnp.dot(collect, dealt, precision=EXACT)

    both = jnp.concatenate(
        [flows.reshape(n_z, own, scens), collected.reshape(n_z, depth // n_z, scens)], axis=1
    )
    height = own + depth // n_z
    summed = jnp.sum(exchange(both.reshape(n_z * height, scens), "z").reshape(n_z, height, scens), axis=0)
    base = summed[:own]
    class_flow = gather_all(summed[own:], "z", n_z)
    outage_flow = gather_all(class_flow, PLANE, n_plane)

    gain = (0.5 / (softness * ratings))[:, None]
    local = overload_sums(where, outage_flow, base, lodf, gain)
    total = local + lax.ppermute(local, "scen", [(0, 1), (1, 0)])
    return 0.5 + total * (0.5 / (scens * lax.axis_size("scen")))


def solution(mesh):
    n_line, n_bus, n_scen = (mesh.shape[name] for name in ("line", "bus", "scen"))
    split = Mesh(
        mesh.devices.reshape(n_line, 2, n_bus // 2, n_scen), ("line", "yl", "z", "scen")
    )
    return jax.shard_map(
        shards,
        mesh=split,
        in_specs=(
            P("line", ("yl", "z")),
            P(("yl", "z"), "scen"),
            P(("line", "yl", "z"), None),
            P(("line", "yl", "z")),
            P(),
        ),
        out_specs=P(("line", "yl", "z"), None),
        check_vma=False,
    )
```

time: 667 us -> 183 us (0.27)
  waiting for transfers between devices: 585 us -> 37.7 us
  blocking collectives: 0 us -> 67.1 us
  other arithmetic: 47.3 us -> 9.69 us
  Pallas kernels: 0 us -> 28.6 us
  starting transfers between devices: 0.09 us -> 26.7 us
  between operations: 13.2 us -> 0.19 us
  local copies, waits for them, and re-layouts: 18.2 us -> 7.1 us
    psum x2 -> x0, waiting for transfers between devices: 466 us -> none  [the longest x1 420 us: shards(): lax.psum(select_rows(base_flow, outages, first_own), ('line', 'bus'))]
    reduce_scatter x1 -> x0, waiting for transfers between devices: 118 us -> none  [shards(): lax.psum_scatter(jnp.dot(ptdf, injections, preferred_element_type=jnp.flo...]
    all_to_all x0 -> x2, blocking collectives: none -> 67.1 us  [exchange(): return lax.all_to_all(values, axes, 0, 0, tiled=True)]
    reduce_sum x8 -> x5, other arithmetic: 41.2 us -> 4.82 us  [the longest x1 1.8 us: shards(): jnp.sum((outages[None, :] < outages[:, None]).astype(jnp.int32), axis=1)]
    all_to_all x0 -> x2, waiting for transfers between devices: none -> 32.1 us  [exchange(): return lax.all_to_all(values, axes, 0, 0, tiled=True)]
    pallas_call x0 -> x1, Pallas kernels: none -> 28.6 us  [overload_sums(): pl.pallas_call(overload_kernel, out_shape=jax.ShapeDtypeStruct((lines, ou...]
    all_to_all x0 -> x2, starting transfers between devices: none -> 15.9 us  [exchange(): return lax.all_to_all(values, axes, 0, 0, tiled=True)]
    ppermute x0 -> x2, starting transfers between devices: none -> 10.7 us  [the longest x1 6.72 us: shards(): total = local + lax.ppermute(local, 'scen', [(0, 1), (1, 0)])]
  transfers between devices with their start and end apart: 3 -> 4, of which waited for: 3 -> 4; matrix products, arithmetic and copies ran while one was open for 0% -> 4% of each run, Pallas kernels for 0% -> 0%
where the time goes in v1:
time: 183 us; the launch traced here: 182 us
  blocking collectives  67.1 us (37%)
  waiting for transfers between devices  37.7 us (21%)
  Pallas kernels  28.6 us (16%)
  starting transfers between devices  26.7 us (15%)
  other arithmetic  9.69 us (5%)
  local copies, waits for them, and re-layouts  7.1 us (4%)
  matrix products  5 us (3%)
    all_to_all x2, blocking collectives, exchange(): return lax.all_to_all(values, axes, 0, 0, tiled=True)  67.1 us
    all_to_all x2, waiting for transfers between devices, exchange(): return lax.all_to_all(values, axes, 0, 0, tiled=True)  32.1 us
    pallas_call x1, Pallas kernels, overload_sums(): pl.pallas_call(overload_kernel, out_shape=jax.ShapeDtypeStruct((lines, ou...  28.6 us
    all_to_all x2, starting transfers between devices, exchange(): return lax.all_to_all(values, axes, 0, 0, tiled=True)  15.9 us
    ppermute x1, starting transfers between devices, shards(): total = local + lax.ppermute(local, 'scen', [(0, 1), (1, 0)])  6.72 us
    ppermute x1, waiting for transfers between devices, shards(): flows = kept + lax.ppermute(sent, 'yl', [(0, 1), (1, 0)])  4.44 us
    unnamed x13, local copies, waits for them, and re-layouts  4.42 us
    ppermute x1, starting transfers between devices, shards(): flows = kept + lax.ppermute(sent, 'yl', [(0, 1), (1, 0)])  4.01 us
  transfers between devices with their start and end apart: 4, of which 4 were waited for; matrix products, arithmetic and copies ran while one was open for 4% of the time, Pallas kernels for 0%

profile of v1, /device:TPU:1, one launch (start us, length us, event | category | flops | bytes accessed | tf_op | source)
XLA Modules:
  0.0 182.0 jit_solution(4895782818532792845)
XLA Ops:
  0.0 1.9 %copy-done = bf16[1024,1536]{1,0:T(8,128)(2,1)S(1)} copy-done((bf16[1024,1536]{1,0:T(8,128)(2,1)S(1)}, bf16[1024,1536]{1,0:T(8,128)(2,1)}, u32[]{:S(2)}) %copy-start) | copy-done | bytes 3145752
  1.9 2.1 %fusion.23 = f32[1024,256]{1,0:T(8,128)S(1)} fusion(bf16[1024,1536]{1,0:T(8,128)(2,1)S(1)} %copy-done, bf16[1536,256]{1,0:T(8,128)(2,1)} %param.6), kind=kOutput, calls=%fused_computation.61 | convolution fusion | flops 805306368 | bytes 4980736 | tf_op jit(solution)/shard_map/dot_general | solution.py:106
  4.0 1.0 copy-done.3
  5.0 0.8 constant_dynamic-slice_fusion
  5.9 4.0 %collective-permute-start = (f32[512,256]{1,0:T(8,128)}, f32[512,256]{1,0:T(8,128)}, u32[]{:S(2)}, u32[]{:S(2)}) collective-permute-start(f32[512,256]{1,0:T(8,128)} %constant_dynamic-slice_fusion), channel_id=1, source_target_pairs={{0,32},{32,0},{1,33},{33,1},{2,34},{34,2},{3,35},{35,3},{4,36},{36... | collective-permute-start | bytes 1572872 | tf_op jit(solution)/shard_map/ppermute | solution.py:110
  9.9 0.6 convert_reduce_fusion.4
  10.6 1.1 convert_reduce_fusion.2
  11.6 0.2 convert_reduce_fusion.3
  11.9 0.7 fusion.17
  12.6 4.4 %collective-permute-done = f32[512,256]{1,0:T(8,128)} collective-permute-done((f32[512,256]{1,0:T(8,128)}, f32[512,256]{1,0:T(8,128)}, u32[]{:S(2)}, u32[]{:S(2)}) %collective-permute-start) | collective-permute-done | bytes 524320 | tf_op jit(solution)/shard_map/ppermute | solution.py:110
  17.0 1.3 dynamic-slice_add_fusion
  18.3 0.8 copy-done.2
  19.1 1.5 fusion
  20.5 11.5 %all-to-all-start = ((f32[16,32,256]{2,1,0:T(8,128)}), f32[16,32,256]{2,1,0:T(8,128)}, u32[]{:S(2)}, u32[]{:S(2)}) async-start(f32[16,32,256]{2,1,0:T(8,128)} %bitcast.16), calls=%async_computation | async-start | bytes 1048576 | tf_op jit(solution)/shard_map/all_to_all | solution.py:90
  32.3 0.1 lt.83
  32.4 9.8 %all-to-all-done = f32[16,32,256]{2,1,0:T(8,128)} async-done(((f32[16,32,256]{2,1,0:T(8,128)}), f32[16,32,256]{2,1,0:T(8,128)}, u32[]{:S(2)}, u32[]{:S(2)}) %all-to-all-start) | async-done | bytes 524320 | tf_op jit(solution)/shard_map/all_to_all | solution.py:90
  42.2 1.4 fusion.2
  43.6 1.1 pad_maximum_fusion
  44.7 48.4 %all_to_all.32 = f32[16,40,256]{2,1,0:T(8,128)} all-to-all(f32[16,40,256]{2,1,0:T(8,128)S(1)} %pad_maximum_fusion), channel_id=1, replica_groups=mesh['line'=8,'yl'=2,'z'=16,'scen'=2] {'z'}, dimensions={0} | all-to-all | bytes 1310720 | tf_op jit(solution)/shard_map/all_to_all | solution.py:90
  93.2 1.1 reduce_sum.59
  94.3 18.6 %all_to_all.33 = f32[16,8,256]{2,1,0:T(8,128)S(1)} all-to-all(f32[16,8,256]{2,1,0:T(8,128)S(1)} %tile.6), channel_id=1, replica_groups=mesh['line'=8,'yl'=2,'z'=16,'scen'=2] {'z'}, dimensions={0} | all-to-all | bytes 262144 | tf_op jit(solution)/shard_map/all_to_all | solution.py:90
  113.0 1.5 tile.8
  114.5 4.4 %all-to-all-start.3 = ((f32[16,128,256]{2,1,0:T(8,128)}), f32[16,128,256]{2,1,0:T(8,128)}, u32[]{:S(2)}, u32[]{:S(2)}) async-start(f32[16,128,256]{2,1,0:T(8,128)} %tile.8), calls=%async_computation.3 | async-start | bytes 4194304 | tf_op jit(solution)/shard_map/all_to_all | solution.py:90
  118.9 0.1 copy.11.gain_ref
  119.0 1.8 convert_reduce_fusion
  120.9 0.8 copy.12
  121.6 0.9 multiply_bitcast_fusion.base_ref
  122.5 22.3 %all-to-all-done.3 = f32[16,128,256]{2,1,0:T(8,128)} async-done(((f32[16,128,256]{2,1,0:T(8,128)}), f32[16,128,256]{2,1,0:T(8,128)}, u32[]{:S(2)}, u32[]{:S(2)}) %all-to-all-start.3) | async-done | bytes 2097184 | tf_op jit(solution)/shard_map/all_to_all | solution.py:90
  144.8 28.6 %shard_map.55 = f32[32,2048]{1,0:T(8,128)S(1)} custom-call(s32[2048]{0:T(1024)S(1)} %fusion.7.where_ref, f32[2048,256]{1,0:T(8,128)} %bitcast.5.flow_ref, f32[256,32]{1,0:T(8,128)S(1)} %multiply_bitcast_fusion.base_ref, bf16[32,2048]{1,0:T(8,128)(2,1)S(1)} %copy-done.1, f32[32,1]{1,0:T(8,128)S(1)} %copy.11.gain_ref), custom_call_target="tpu_custom_call" | custom-call | flops 83886080 | bytes 2490368 | tf_op jit(solution)/shard_map/pallas_call | solution.py:60
  173.4 6.7 %collective-permute-start.1 = (f32[32,2048]{1,0:T(8,128)S(1)}, f32[32,2048]{1,0:T(8,128)S(1)}, u32[]{:S(2)}, u32[]{:S(2)}) collective-permute-start(f32[32,2048]{1,0:T(8,128)S(1)} %shard_map.55), channel_id=1, source_target_pairs={{0,1},{1,0},{2,3},{3,2},{4,5},{5,4},{6,7},{7,6},{8,9},{9,8},{10,11... | collective-permute-start | bytes 786440 | tf_op jit(solution)/shard_map/ppermute | solution.py:142
  180.1 1.1 collective-permute-done.1
  181.2 0.7 multiply_add_fusion
  (24 shorter events, 0.4 us)
Async XLA Ops:
  0.0 1.9 %copy-start = (bf16[1024,1536]{1,0:T(8,128)(2,1)S(1)}, bf16[1024,1536]{1,0:T(8,128)(2,1)}, u32[]{:S(2)}) copy-start(bf16[1024,1536]{1,0:T(8,128)(2,1)} %param.5) | copy-start | bytes 9437188
  1.9 8.0 %copy-start.4 = (s32[2048]{0:T(1024)S(1)}, s32[2048]{0:T(1024)}, u32[]{:S(2)}) copy-start(s32[2048]{0:T(1024)} %param.9) | copy-start | bytes 24580
  4.0 1.0 copy-start.3
  5.9 11.1 %collective-permute-start = (f32[512,256]{1,0:T(8,128)}, f32[512,256]{1,0:T(8,128)}, u32[]{:S(2)}, u32[]{:S(2)}) collective-permute-start(f32[512,256]{1,0:T(8,128)} %constant_dynamic-slice_fusion), channel_id=1, source_target_pairs={{0,32},{32,0},{1,33},{33,1},{2,34},{34,2},{3,35},{35,3},{4,36},{36... | collective-permute-start | bytes 1572872 | tf_op jit(solution)/shard_map/ppermute | solution.py:110
  18.3 0.8 copy-start.2
  20.5 21.7 %all-to-all-start = ((f32[16,32,256]{2,1,0:T(8,128)}), f32[16,32,256]{2,1,0:T(8,128)}, u32[]{:S(2)}, u32[]{:S(2)}) async-start(f32[16,32,256]{2,1,0:T(8,128)} %bitcast.16), calls=%async_computation | async-start | bytes 1048576 | tf_op jit(solution)/shard_map/all_to_all | solution.py:90
  113.0 5.9 %copy-start.5 = (f32[32]{0:T(128)S(1)}, f32[32]{0:T(128)}, u32[]{:S(2)}) copy-start(f32[32]{0:T(128)} %param.8) | copy-start | bytes 388
  113.0 31.8 %copy-start.1 = (bf16[32,2048]{1,0:T(8,128)(2,1)S(1)}, bf16[32,2048]{1,0:T(8,128)(2,1)}, u32[]{:S(2)}) copy-start(bf16[32,2048]{1,0:T(8,128)(2,1)} %lodf_ref.1) | copy-start | bytes 393220
  114.5 30.3 %all-to-all-start.3 = ((f32[16,128,256]{2,1,0:T(8,128)}), f32[16,128,256]{2,1,0:T(8,128)}, u32[]{:S(2)}, u32[]{:S(2)}) async-start(f32[16,128,256]{2,1,0:T(8,128)} %tile.8), calls=%async_computation.3 | async-start | bytes 4194304 | tf_op jit(solution)/shard_map/all_to_all | solution.py:90
  173.4 7.9 %collective-permute-start.1 = (f32[32,2048]{1,0:T(8,128)S(1)}, f32[32,2048]{1,0:T(8,128)S(1)}, u32[]{:S(2)}, u32[]{:S(2)}) collective-permute-start(f32[32,2048]{1,0:T(8,128)S(1)} %shard_map.55), channel_id=1, source_target_pairs={{0,1},{1,0},{2,3},{3,2},{4,5},{5,4},{6,7},{7,6},{8,9},{9,8},{10,11... | collective-permute-start | bytes 786440 | tf_op jit(solution)/shard_map/ppermute | solution.py:142

commit v2 on v1

v2 whole, which is shorter than its diff:
```python
import jax
import jax.numpy as jnp
from jax import lax
from jax.experimental import pallas as pl
from jax.experimental.pallas import tpu as pltpu
from jax.sharding import Mesh, PartitionSpec as P

softness = 0.2
PLANE = ("line", "yl")
PARTS = 2


def overload_kernel(where_ref, flow_ref, base_ref, lodf_ref, gain_ref, out_ref, spread, rows, turned, scaled):
    lines, scens = base_ref.shape[1], base_ref.shape[0]
    tile = out_ref.shape[1]
    step = pl.program_id(0)
    trips = lines // 2
    per_trip = tile // trips

    def fetch(from_step, first, number):
        for offset in range(number):
            slot = first + offset
            rows[pl.ds(slot, 1), :] = flow_ref[pl.ds(where_ref[from_step * tile + slot], 1), :]

    @pl.when(step == 0)
    def _():
        for line in range(lines):
            spread[line] = jnp.broadcast_to(base_ref[:, line : line + 1], (scens, 128))

        def some(group, carry):
            fetch(0, group * 16, 16)
            return carry

        lax.fori_loop(0, tile // 16, some, 0)

    for part in range(tile // 128):
        turned[:, part * 128 : part * 128 + 128] = rows[part * 128 : part * 128 + 128, :].T
    scaled[...] = lodf_ref[...].astype(jnp.float32) * gain_ref[...]
    ahead = jnp.minimum(step + 1, pl.num_programs(0) - 1)

    def pair(index, carry):
        first = index * 2
        factors = []
        for j in range(2):
            row = scaled[pl.ds(first + j, 1), :]
            factors.append([jnp.broadcast_to(row[:, k : k + 128], (8, 128)) for k in range(0, tile, 128)])
        sums = [[jnp.zeros((8, 128), jnp.float32) for _ in range(0, tile, 128)] for j in range(2)]
        fetch(ahead, index * per_trip, per_trip)
        for s in range(0, scens, 8):
            levels = [spread[first + j, s : s + 8, :] for j in range(2)]
            for part in range(tile // 128):
                flow = turned[s : s + 8, part * 128 : part * 128 + 128]
                for j in range(2):
                    level = levels[j] + factors[j][part] * flow
                    sums[j][part] = sums[j][part] + jnp.tanh(jnp.abs(level) - 0.5 / softness)
        for j in range(2):
            out_ref[pl.ds(first + j, 1), :] = jnp.concatenate(
                [jnp.sum(total, axis=0, keepdims=True) for total in sums[j]], axis=1
            )
        return carry

    lax.fori_loop(0, trips, pair, 0)


def overload_sums(where, flow, base, lodf, gain, part):
    lines = lodf.shape[0]
    outages, scens = flow.shape
    tile = min(256, outages)
    ahead = part * (outages // tile)
    return pl.pallas_call(
        overload_kernel,
        out_shape=jax.ShapeDtypeStruct((lines, outages), jnp.float32),
        grid_spec=pltpu.PrefetchScalarGridSpec(
            num_scalar_prefetch=1,
            grid=(outages // tile,),
            in_specs=[
                pl.BlockSpec((outages, scens), lambda i, w: (0, 0), pipeline_mode=pl.Buffered(1)),
                pl.BlockSpec((scens, lines), lambda i, w: (0, 0), pipeline_mode=pl.Buffered(1)),
                pl.BlockSpec((lines, tile), lambda i, w: (0, i + ahead)),
                pl.BlockSpec((lines, 1), lambda i, w: (0, 0), pipeline_mode=pl.Buffered(1)),
            ],
            out_specs=pl.BlockSpec((lines, tile), lambda i, w: (0, i)),
            scratch_shapes=[
                pltpu.VMEM((lines, scens, 128), jnp.float32),
                pltpu.VMEM((tile, scens), jnp.float32),
                pltpu.VMEM((scens, tile), jnp.float32),
                pltpu.VMEM((lines, tile), jnp.float32),
            ],
        ),
        compiler_params=pltpu.CompilerParams(vmem_limit_bytes=16 << 20),
        cost_estimate=pl.CostEstimate(
            flops=5 * lines * outages * scens,
            transcendentals=lines * outages * scens,
            bytes_accessed=4 * outages * scens + 6 * lines * outages,
        ),
    )(where, flow, base, lodf, gain)


def exchange(values, axes):
    return lax.all_to_all(values, axes, 0, 0, tiled=True)


def gather_all(rows, axes, members):
    return exchange(jnp.tile(rows, (members, 1)), axes)


def select(choice, values):
    high = lax.reduce_precision(values, 8, 7)
    rest = values - high
    middle = lax.reduce_precision(rest, 8, 7)
    pieces = [piece.astype(jnp.bfloat16) for piece in (high, middle, rest - middle)]
    picked = jnp.dot(
        choice.astype(jnp.bfloat16), jnp.concatenate(pieces, axis=1), preferred_element_type=jnp.float32
    )
    width = values.shape[1]
    return picked[:, :width] + (picked[:, width : 2 * width] + picked[:, 2 * width :])


def halve(rows, axis, bit):
    mine = (lax.axis_index(axis) // bit) % 2
    pairs = [(member, member ^ bit) for member in range(lax.axis_size(axis))]
    sent = lax.dynamic_slice_in_dim(rows, 1 - mine, 1, axis=1)
    return lax.dynamic_slice_in_dim(rows, mine, 1, axis=1) + lax.ppermute(sent, axis, pairs)


def below(outages, limits):
    return jnp.sum((outages[None, :] < limits[:, None]).astype(jnp.int32), axis=1)


def shards(ptdf, injections, lodf, ratings, outages):
    own, count = lodf.shape
    scens = injections.shape[1]
    n_line, n_yl, n_z = (lax.axis_size(name) for name in ("line", "yl", "z"))
    n_class = n_line * n_yl
    line, yl = lax.axis_index("line"), lax.axis_index("yl")
    group = ptdf.shape[0]
    column = group // n_yl
    depth = count // PARTS // n_class
    share = -(-(-(-group // n_class) + PARTS) // 8) * 8

    partial = jnp.dot(ptdf, injections, preferred_element_type=jnp.float32)

    pieces = [outages[part * (count // PARTS) : (part + 1) * (count // PARTS)] for part in range(PARTS)]
    edges = group * jnp.arange(n_line + 1)
    lines = line * group + jnp.arange(group)
    slot = jnp.full((group,), -1, jnp.int32)
    used = jnp.zeros((n_line,), jnp.int32)
    here = line * n_yl + yl
    places = jnp.arange(share)[None, :]
    source_row = jnp.full((n_line, share), -1, jnp.int32)
    for part, piece in enumerate(pieces):
        starts = below(piece, edges)
        first, number = starts[:-1], starts[1:] - starts[:-1]
        before, through = below(piece, lines), below(piece, lines + 1)
        mine = before - jnp.sum(jnp.where(jnp.arange(n_line) == line, first, 0))
        offset = jnp.sum(jnp.where(jnp.arange(n_line) == line, used, 0))
        slot = jnp.where(through > before, (before % n_class) * share + offset + mine // n_class, slot)
        turn = places - used[:, None]
        nth = lax.rem(here - first + count * n_class, n_class)[:, None] + n_class * turn
        found = (turn >= 0) & (nth < number[:, None])
        source_row = jnp.where(found, part * depth + (first[:, None] + nth) // n_class, source_row)
        used = used + (number + n_class - 1) // n_class

    deal = slot[None, :] == jnp.arange(n_class * share)[:, None]
    to_classes = select(deal, partial)
    dealt = exchange(to_classes, PLANE)
    to_classes, outages = lax.optimization_barrier((to_classes, outages))
    wheres = []
    for part in range(PARTS):
        piece = outages[part * (count // PARTS) : (part + 1) * (count // PARTS)]
        rank = below(piece, piece)
        wheres.append((rank % n_class) * depth + rank // n_class)
    source_row = jnp.broadcast_to(source_row[:, None, :], (n_line, n_yl, share)).reshape(-1)
    collect = source_row[None, :] == jnp.arange(PARTS * depth)[:, None]
    collected = select(collect, dealt)

    base = halve(partial.reshape(1, n_yl, column, scens), "yl", 1)
    spans = [1 << bit for bit in range(n_z.bit_length() - 1)]

    def halved(base, count):
        for span in [spans.pop(0) for _ in range(min(count, len(spans)))]:
            base = halve(base.reshape(n_z // span // 2, 2, own, scens), "z", span)
        return base

    collected, base = lax.optimization_barrier((collected, halved(base, 1)))
    class_flow = jnp.sum(exchange(collected, "z").reshape(n_z, -1, scens), axis=0)
    class_flow, base = lax.optimization_barrier((class_flow, halved(base, 1)))
    class_flow = gather_all(class_flow, "z", n_z)
    class_flow, base = lax.optimization_barrier((class_flow, halved(base, 1)))
    base = halved(base, len(spans))
    flows = []
    for part in range(PARTS):
        rows = class_flow[part * depth : (part + 1) * depth]
        if part:
            rows, base = lax.optimization_barrier((rows, base))
        flows.append(gather_all(rows, PLANE, n_class))
    base = base.reshape(own, scens)

    gain = (0.5 / (softness * ratings))[:, None]
    scaled_base = (base * gain).T
    totals = []
    for part in range(PARTS):
        local = overload_sums(wheres[part], flows[part], scaled_base, lodf, gain, part)
        totals.append(local + lax.ppermute(local, "scen", [(0, 1), (1, 0)]))
    return 0.5 + jnp.concatenate(totals, axis=1) * (0.5 / (scens * lax.axis_size("scen")))


def solution(mesh):
    n_line, n_bus, n_scen = (mesh.shape[name] for name in ("line", "bus", "scen"))
    split = Mesh(
        mesh.devices.reshape(n_line, 2, n_bus // 2, n_scen), ("line", "yl", "z", "scen")
    )
    return jax.shard_map(
        shards,
        mesh=split,
        in_specs=(
            P("line", ("yl", "z")),
            P(("yl", "z"), "scen"),
            P(("line", "yl", "z"), None),
            P(("line", "yl", "z")),
            P(),
        ),
        out_specs=P(("line", "yl", "z"), None),
        check_vma=False,
    )
```

time: 183 us -> 205 us (1.12)
  blocking collectives: 67.1 us -> 0 us
  starting transfers between devices: 26.7 us -> 77.8 us
  waiting for transfers between devices: 37.7 us -> 55.4 us
  other arithmetic: 9.69 us -> 18.2 us
  local copies, waits for them, and re-layouts: 7.1 us -> 12.9 us
  Pallas kernels: 28.6 us -> 31.5 us
  matrix products: 5 us -> 7.27 us
    all_to_all x2 -> x0, blocking collectives: 67.1 us -> none  [exchange(): return lax.all_to_all(values, axes, 0, 0, tiled=True)]
    ppermute x2 -> x7, waiting for transfers between devices: 5.58 us -> 50.1 us  [the longest x5 49.7 us: halve(): lax.ppermute(sent, axis, pairs)]
    all_to_all x2 -> x5, starting transfers between devices: 15.9 us -> 44.7 us  [exchange(): return lax.all_to_all(values, axes, 0, 0, tiled=True)]
    all_to_all x2 -> x5, waiting for transfers between devices: 32.1 us -> 5.31 us  [exchange(): return lax.all_to_all(values, axes, 0, 0, tiled=True)]
    ppermute x2 -> x7, starting transfers between devices: 10.7 us -> 33.1 us  [the longest x5 28.5 us: halve(): lax.ppermute(sent, axis, pairs)]
    add x5 -> x13, other arithmetic: 2.1 us -> 9.55 us  [the longest x5 5.89 us: halve(): lax.dynamic_slice_in_dim(rows, mine, 1, axis=1)]
    pallas_call x1 -> x2, Pallas kernels: 28.6 us -> 31.5 us  [overload_sums(): pl.pallas_call(overload_kernel, out_shape=jax.ShapeDtypeStruct((lines, ou...]
    unnamed x13 -> x16, local copies, waits for them, and re-layouts: 4.42 us -> 5.47 us
  transfers between devices with their start and end apart: 4 -> 12, of which waited for: 4 -> 6; matrix products, arithmetic and copies ran while one was open for 4% -> 10% of each run, Pallas kernels for 0% -> 15%
where the time goes in v2:
time: 205 us; the launch traced here: 204 us
  starting transfers between devices  77.8 us (38%)
  waiting for transfers between devices  55.4 us (27%)
  Pallas kernels  31.5 us (15%)
  other arithmetic  18.2 us (9%)
  local copies, waits for them, and re-layouts  12.9 us (6%)
  matrix products  7.27 us (4%)
    ppermute x5, waiting for transfers between devices, halve(): lax.ppermute(sent, axis, pairs)  49.7 us
    all_to_all x5, starting transfers between devices, exchange(): return lax.all_to_all(values, axes, 0, 0, tiled=True)  44.7 us
    pallas_call x2, Pallas kernels, overload_sums(): pl.pallas_call(overload_kernel, out_shape=jax.ShapeDtypeStruct((lines, ou...  31.5 us
    ppermute x5, starting transfers between devices, halve(): lax.ppermute(sent, axis, pairs)  28.5 us
    add x5, other arithmetic, halve(): lax.dynamic_slice_in_dim(rows, mine, 1, axis=1)  5.89 us
    unnamed x16, local copies, waits for them, and re-layouts  5.47 us
    all_to_all x5, waiting for transfers between devices, exchange(): return lax.all_to_all(values, axes, 0, 0, tiled=True)  5.31 us
    ppermute x2, starting transfers between devices, shards(): totals.append(local + lax.ppermute(local, 'scen', [(0, 1), (1, 0)]))  4.6 us
  transfers between devices with their start and end apart: 12, of which 6 were waited for; matrix products, arithmetic and copies ran while one was open for 10% of the time, Pallas kernels for 15%

profile of v2, /device:TPU:1, one launch (start us, length us, event | category | flops | bytes accessed | tf_op | source)
XLA Modules:
  0.0 203.6 jit_solution(5215867112028459968)
XLA Ops:
  0.0 1.9 copy-done
  1.9 3.3 %reduce-precision_convert_fusion.3 = (bf16[1024,256]{1,0:T(8,128)(2,1)}, bf16[1024,256]{1,0:T(8,128)(2,1)}, bf16[1024,256]{1,0:T(8,128)(2,1)}, f32[1024,256]{1,0:T(8,128)S(1)}) fusion(bf16[1024,1536]{1,0:T(8,128)(2,1)S(1)} %copy-done, bf16[1536,256]{1,0:T(8,128)(2,1)} %param.6), kind=kOutput, calls=%fused_computation.27 | convolution fusion | flops 807141376 | bytes 6553600 | tf_op jit(solution)/shard_map/dot_general | solution.py:141
  7.0 4.0 %collective-permute-start = (f32[1,1,512,256]{3,2,1,0:T(8,128)}, f32[1,1,512,256]{3,2,1,0:T(8,128)}, u32[]{:S(2)}, u32[]{:S(2)}) collective-permute-start(f32[1,1,512,256]{3,2,1,0:T(8,128)} %constant_dynamic-slice_fusion.4), channel_id=1, source_target_pairs={{0,32},{32,0},{1,33},{33,1},{2,34},{34,2},{3,35},{35,3},{4,36},{36... | collective-permute-start | bytes 1572872 | tf_op jit(solution)/shard_map/ppermute | solution.py:123
  11.2 2.1 %convert_reduce_fusion.5 = (s32[1024]{0:T(1024)S(1)}, s32[1024]{0:T(1024)S(1)}, s32[1024]{0:T(1024)S(1)}, s32[1024]{0:T(1024)S(1)}) fusion(s32[1024]{0:T(1024)S(1)} %get-tuple-element.43, s32[1024]{0:T(1024)S(1)} %get-tuple-element.60, s32[1024]{0:T(1024)S(1)} %get-tuple-element.42, s32[1024]{0:T(1024)S(1)} %get-tuple-element.59), kind=kLoop, calls=%fused_computation.7 | loop fusion | flops 12578816 | bytes 32768 | tf_op jit(solution)/shard_map/reduce_sum | solution.py:127
  14.1 1.9 fusion.29
  16.0 3.5 %fusion = f32[1152,768]{1,0:T(8,128)S(1)} fusion(s32[1024]{0:T(1024)S(1)} %fusion.29, bf16[1024,256]{1,0:T(8,128)(2,1)} %get-tuple-element.36, bf16[1024,256]{1,0:T(8,128)(2,1)} %get-tuple-element.37, bf16[1024,256]{1,0:T(8,128)(2,1)} %get-tuple-element.35), kind=kOutput, calls=%fused_computation.1 | convolution fusion | flops 1817837568 | bytes 5115904 | tf_op jit(solution)/shard_map/dot_general | solution.py:112
  19.6 1.3 fusion.14
  20.8 6.5 %all-to-all-start = ((f32[16,72,256]{2,1,0:T(8,128)}), f32[16,72,256]{2,1,0:T(8,128)}, u32[]{:S(2)}, u32[]{:S(2)}) async-start(f32[16,72,256]{2,1,0:T(8,128)} %bitcast.26), calls=%async_computation | async-start | bytes 2359296 | tf_op jit(solution)/shard_map/all_to_all | solution.py:100
  27.4 1.3 dynamic-slice_add_fusion
  29.5 3.6 %collective-permute-start.1 = (f32[8,1,32,256]{3,2,1,0:T(8,128)S(1)}, f32[8,1,32,256]{3,2,1,0:T(8,128)}, u32[]{:S(2)}, u32[]{:S(2)}) collective-permute-start(f32[8,1,32,256]{3,2,1,0:T(8,128)S(1)} %constant_dynamic-slice_fusion.3), channel_id=1, source_target_pairs={{0,2},{2,0},{4,6},{6,4},{8,10},{10,8},{12,14},{14,12},{16,18},{18,... | collective-permute-start | bytes 786440 | tf_op jit(solution)/shard_map/ppermute | solution.py:123
  33.3 4.2 %collective-permute-done.1 = f32[8,1,32,256]{3,2,1,0:T(8,128)} collective-permute-done((f32[8,1,32,256]{3,2,1,0:T(8,128)S(1)}, f32[8,1,32,256]{3,2,1,0:T(8,128)}, u32[]{:S(2)}, u32[]{:S(2)}) %collective-permute-start.1) | collective-permute-done | bytes 262176 | tf_op jit(solution)/shard_map/ppermute | solution.py:123
  37.5 1.1 dynamic-slice_add_fusion.2
  38.5 5.3 %all-to-all-done = f32[16,72,256]{2,1,0:T(8,128)} async-done(((f32[16,72,256]{2,1,0:T(8,128)}), f32[16,72,256]{2,1,0:T(8,128)}, u32[]{:S(2)}, u32[]{:S(2)}) %all-to-all-start) | async-done | bytes 1179680 | tf_op jit(solution)/shard_map/all_to_all | solution.py:100
  43.8 1.5 reduce-precision_convert_fusion.1
  46.5 15.9 %all-to-all-start.1 = ((f32[16,8,256]{2,1,0:T(8,128)}), f32[16,8,256]{2,1,0:T(8,128)}, u32[]{:S(2)}, u32[]{:S(2)}) async-start(f32[16,8,256]{2,1,0:T(8,128)} %bitcast.4), calls=%async_computation.1 | async-start | bytes 262144 | tf_op jit(solution)/shard_map/all_to_all | solution.py:100
  62.5 4.1 %collective-permute-start.2 = (f32[4,1,32,256]{3,2,1,0:T(8,128)S(1)}, f32[4,1,32,256]{3,2,1,0:T(8,128)}, u32[]{:S(2)}, u32[]{:S(2)}) collective-permute-start(f32[4,1,32,256]{3,2,1,0:T(8,128)S(1)} %constant_dynamic-slice_fusion.2), channel_id=1, source_target_pairs={{0,4},{2,6},{4,0},{6,2},{8,12},{10,14},{12,8},{14,10},{16,20},{18,... | collective-permute-start | bytes 393224 | tf_op jit(solution)/shard_map/ppermute | solution.py:123
  66.6 9.1 %collective-permute-done.2 = f32[4,1,32,256]{3,2,1,0:T(8,128)} collective-permute-done((f32[4,1,32,256]{3,2,1,0:T(8,128)S(1)}, f32[4,1,32,256]{3,2,1,0:T(8,128)}, u32[]{:S(2)}, u32[]{:S(2)}) %collective-permute-start.2) | collective-permute-done | bytes 131104 | tf_op jit(solution)/shard_map/ppermute | solution.py:123
  78.2 11.4 %all-to-all-start.2 = ((f32[16,8,256]{2,1,0:T(8,128)}), f32[16,8,256]{2,1,0:T(8,128)}, u32[]{:S(2)}, u32[]{:S(2)}) async-start(f32[16,8,256]{2,1,0:T(8,128)} %tile.6), calls=%async_computation.2 | async-start | bytes 262144 | tf_op jit(solution)/shard_map/all_to_all | solution.py:100
  91.6 7.1 %collective-permute-start.3 = (f32[2,1,32,256]{2,3,1,0:T(8,128)S(1)}, f32[2,1,32,256]{2,3,1,0:T(8,128)}, u32[]{:S(2)}, u32[]{:S(2)}) collective-permute-start(f32[2,1,32,256]{2,3,1,0:T(8,128)S(1)} %constant_dynamic-slice_fusion.1), channel_id=1, source_target_pairs={{0,8},{2,10},{4,12},{6,14},{8,0},{10,2},{12,4},{14,6},{16,24},{18,... | collective-permute-start | bytes 196616 | tf_op jit(solution)/shard_map/ppermute | solution.py:123
  98.7 26.0 %collective-permute-done.3 = f32[2,1,32,256]{2,3,1,0:T(8,128)} collective-permute-done((f32[2,1,32,256]{2,3,1,0:T(8,128)S(1)}, f32[2,1,32,256]{2,3,1,0:T(8,128)}, u32[]{:S(2)}, u32[]{:S(2)}) %collective-permute-start.3) | collective-permute-done | bytes 65568 | tf_op jit(solution)/shard_map/ppermute | solution.py:123
  124.7 1.1 dynamic-slice_add_fusion.1
  126.7 1.1 tile.7
  127.8 4.3 %all-to-all-start.3 = ((f32[16,64,256]{2,1,0:T(8,128)}), f32[16,64,256]{2,1,0:T(8,128)}, u32[]{:S(2)}, u32[]{:S(2)}) async-start(f32[16,64,256]{2,1,0:T(8,128)} %tile.7), calls=%async_computation.3 | async-start | bytes 2097152 | tf_op jit(solution)/shard_map/all_to_all | solution.py:100
  132.9 9.8 %collective-permute-start.4 = (f32[1,1,32,256]{2,3,1,0:T(8,128)}, f32[1,1,32,256]{2,3,1,0:T(8,128)}, u32[]{:S(2)}, u32[]{:S(2)}) collective-permute-start(f32[1,1,32,256]{2,3,1,0:T(8,128)} %constant_dynamic-slice_fusion), channel_id=1, source_target_pairs={{0,16},{2,18},{4,20},{6,22},{8,24},{10,26},{12,28},{14,30},{16,0},... | collective-permute-start | bytes 98312 | tf_op jit(solution)/shard_map/ppermute | solution.py:123
  143.3 10.4 %collective-permute-done.4 = f32[1,1,32,256]{2,3,1,0:T(8,128)} collective-permute-done((f32[1,1,32,256]{2,3,1,0:T(8,128)}, f32[1,1,32,256]{2,3,1,0:T(8,128)}, u32[]{:S(2)}, u32[]{:S(2)}) %collective-permute-start.4) | collective-permute-done | bytes 32800 | tf_op jit(solution)/shard_map/ppermute | solution.py:123
  153.7 1.6 dynamic-slice_add_fusion.3
  155.3 1.1 tile.8
  156.4 6.6 %all-to-all-start.4 = ((f32[16,64,256]{2,1,0:T(8,128)}), f32[16,64,256]{2,1,0:T(8,128)}, u32[]{:S(2)}, u32[]{:S(2)}) async-start(f32[16,64,256]{2,1,0:T(8,128)} %tile.8), calls=%async_computation.4 | async-start | bytes 2097152 | tf_op jit(solution)/shard_map/all_to_all | solution.py:100
  164.6 15.7 %shard_map.55 = f32[32,1024]{1,0:T(8,128)S(1)} custom-call(s32[1024]{0:T(1024)S(1)} %fusion.37.where_ref, f32[1024,256]{1,0:T(8,128)} %bitcast.8.flow_ref, f32[256,32]{1,0:T(8,128)S(1)} %fusion.19.base_ref, bf16[32,2048]{1,0:T(8,128)(2,1)S(1)} %copy-done.1, f32[32,1]{1,0:T(8,128)S(1)} %copy.15.gain_ref), custom_call_target="tpu_custom_call" | custom-call | flops 41943040 | bytes 1245184 | tf_op jit(solution)/shard_map/pallas_call | solution.py:70
  180.3 2.7 %collective-permute-start.5 = (f32[32,1024]{1,0:T(8,128)S(1)}, f32[32,1024]{1,0:T(8,128)}, u32[]{:S(2)}, u32[]{:S(2)}) collective-permute-start(f32[32,1024]{1,0:T(8,128)S(1)} %shard_map.55), channel_id=1, source_target_pairs={{0,1},{1,0},{2,3},{3,2},{4,5},{5,4},{6,7},{7,6},{8,9},{9,8},{10,11... | collective-permute-start | bytes 393224 | tf_op jit(solution)/shard_map/ppermute | solution.py:204
  183.9 15.7 %shard_map.56 = f32[32,1024]{1,0:T(8,128)S(1)} custom-call(s32[1024]{0:T(1024)S(1)} %fusion.44.where_ref, f32[1024,256]{1,0:T(8,128)} %bitcast.12.flow_ref, f32[256,32]{1,0:T(8,128)S(1)} %fusion.19.base_ref, bf16[32,2048]{1,0:T(8,128)(2,1)S(1)} %copy-done.2, f32[32,1]{1,0:T(8,128)S(1)} %copy.15.gain_ref), custom_call_target="tpu_custom_call" | custom-call | flops 41943040 | bytes 1245184 | tf_op jit(solution)/shard_map/pallas_call | solution.py:70
  199.6 1.9 collective-permute-start.6
  (55 shorter events, 16.1 us)
Async XLA Ops:
  0.0 1.9 copy-start
  1.9 9.1 %copy-start.6 = (s32[2048]{0:T(1024)S(1)}, s32[2048]{0:T(1024)}, u32[]{:S(2)}) copy-start(s32[2048]{0:T(1024)} %param.9) | copy-start | bytes 24580
  5.2 1.0 copy-start.4
  7.0 20.4 %collective-permute-start = (f32[1,1,512,256]{3,2,1,0:T(8,128)}, f32[1,1,512,256]{3,2,1,0:T(8,128)}, u32[]{:S(2)}, u32[]{:S(2)}) collective-permute-start(f32[1,1,512,256]{3,2,1,0:T(8,128)} %constant_dynamic-slice_fusion.4), channel_id=1, source_target_pairs={{0,32},{32,0},{1,33},{33,1},{2,34},{34,2},{3,35},{35,3},{4,36},{36... | collective-permute-start | bytes 1572872 | tf_op jit(solution)/shard_map/ppermute | solution.py:123
  20.8 23.0 %all-to-all-start = ((f32[16,72,256]{2,1,0:T(8,128)}), f32[16,72,256]{2,1,0:T(8,128)}, u32[]{:S(2)}, u32[]{:S(2)}) async-start(f32[16,72,256]{2,1,0:T(8,128)} %bitcast.26), calls=%async_computation | async-start | bytes 2359296 | tf_op jit(solution)/shard_map/all_to_all | solution.py:100
  28.7 0.8 copy-start.3
  29.5 8.0 %collective-permute-start.1 = (f32[8,1,32,256]{3,2,1,0:T(8,128)S(1)}, f32[8,1,32,256]{3,2,1,0:T(8,128)}, u32[]{:S(2)}, u32[]{:S(2)}) collective-permute-start(f32[8,1,32,256]{3,2,1,0:T(8,128)S(1)} %constant_dynamic-slice_fusion.3), channel_id=1, source_target_pairs={{0,2},{2,0},{4,6},{6,4},{8,10},{10,8},{12,14},{14,12},{16,18},{18,... | collective-permute-start | bytes 786440 | tf_op jit(solution)/shard_map/ppermute | solution.py:123
  46.5 30.1 %all-to-all-start.1 = ((f32[16,8,256]{2,1,0:T(8,128)}), f32[16,8,256]{2,1,0:T(8,128)}, u32[]{:S(2)}, u32[]{:S(2)}) async-start(f32[16,8,256]{2,1,0:T(8,128)} %bitcast.4), calls=%async_computation.1 | async-start | bytes 262144 | tf_op jit(solution)/shard_map/all_to_all | solution.py:100
  62.5 13.2 %collective-permute-start.2 = (f32[4,1,32,256]{3,2,1,0:T(8,128)S(1)}, f32[4,1,32,256]{3,2,1,0:T(8,128)}, u32[]{:S(2)}, u32[]{:S(2)}) collective-permute-start(f32[4,1,32,256]{3,2,1,0:T(8,128)S(1)} %constant_dynamic-slice_fusion.2), channel_id=1, source_target_pairs={{0,4},{2,6},{4,0},{6,2},{8,12},{10,14},{12,8},{14,10},{16,20},{18,... | collective-permute-start | bytes 393224 | tf_op jit(solution)/shard_map/ppermute | solution.py:123
  66.6 65.7 %copy-start.7 = (f32[32]{0:T(128)S(1)}, f32[32]{0:T(128)}, u32[]{:S(2)}) copy-start(f32[32]{0:T(128)} %param.8) | copy-start | bytes 388
  78.2 47.6 %all-to-all-start.2 = ((f32[16,8,256]{2,1,0:T(8,128)}), f32[16,8,256]{2,1,0:T(8,128)}, u32[]{:S(2)}, u32[]{:S(2)}) async-start(f32[16,8,256]{2,1,0:T(8,128)} %tile.6), calls=%async_computation.2 | async-start | bytes 262144 | tf_op jit(solution)/shard_map/all_to_all | solution.py:100
  91.6 33.1 %collective-permute-start.3 = (f32[2,1,32,256]{2,3,1,0:T(8,128)S(1)}, f32[2,1,32,256]{2,3,1,0:T(8,128)}, u32[]{:S(2)}, u32[]{:S(2)}) collective-permute-start(f32[2,1,32,256]{2,3,1,0:T(8,128)S(1)} %constant_dynamic-slice_fusion.1), channel_id=1, source_target_pairs={{0,8},{2,10},{4,12},{6,14},{8,0},{10,2},{12,4},{14,6},{16,24},{18,... | collective-permute-start | bytes 196616 | tf_op jit(solution)/shard_map/ppermute | solution.py:123
  127.8 27.4 %all-to-all-start.3 = ((f32[16,64,256]{2,1,0:T(8,128)}), f32[16,64,256]{2,1,0:T(8,128)}, u32[]{:S(2)}, u32[]{:S(2)}) async-start(f32[16,64,256]{2,1,0:T(8,128)} %tile.7), calls=%async_computation.3 | async-start | bytes 2097152 | tf_op jit(solution)/shard_map/all_to_all | solution.py:100
  132.9 20.8 %collective-permute-start.4 = (f32[1,1,32,256]{2,3,1,0:T(8,128)}, f32[1,1,32,256]{2,3,1,0:T(8,128)}, u32[]{:S(2)}, u32[]{:S(2)}) collective-permute-start(f32[1,1,32,256]{2,3,1,0:T(8,128)} %constant_dynamic-slice_fusion), channel_id=1, source_target_pairs={{0,16},{2,18},{4,20},{6,22},{8,24},{10,26},{12,28},{14,30},{16,0},... | collective-permute-start | bytes 98312 | tf_op jit(solution)/shard_map/ppermute | solution.py:123
  155.3 8.4 %copy-start.5 = (f32[1,1,32,256]{2,3,1,0:T(8,128)S(1)}, f32[1,1,32,256]{2,3,1,0:T(8,128)}, u32[]{:S(2)}) copy-start(f32[1,1,32,256]{2,3,1,0:T(8,128)} %dynamic-slice_add_fusion.3) | copy-start | bytes 98308
  156.4 26.6 %all-to-all-start.4 = ((f32[16,64,256]{2,1,0:T(8,128)}), f32[16,64,256]{2,1,0:T(8,128)}, u32[]{:S(2)}, u32[]{:S(2)}) async-start(f32[16,64,256]{2,1,0:T(8,128)} %tile.8), calls=%async_computation.4 | async-start | bytes 2097152 | tf_op jit(solution)/shard_map/all_to_all | solution.py:100
  163.6 0.9 copy-start.1
  180.3 21.3 %collective-permute-start.5 = (f32[32,1024]{1,0:T(8,128)S(1)}, f32[32,1024]{1,0:T(8,128)}, u32[]{:S(2)}, u32[]{:S(2)}) collective-permute-start(f32[32,1024]{1,0:T(8,128)S(1)} %shard_map.55), channel_id=1, source_target_pairs={{0,1},{1,0},{2,3},{3,2},{4,5},{5,4},{6,7},{7,6},{8,9},{9,8},{10,11... | collective-permute-start | bytes 393224 | tf_op jit(solution)/shard_map/ppermute | solution.py:204
  183.0 0.9 copy-start.2
  199.6 3.2 %collective-permute-start.6 = (f32[32,1024]{1,0:T(8,128)S(1)}, f32[32,1024]{1,0:T(8,128)S(1)}, u32[]{:S(2)}, u32[]{:S(2)}) collective-permute-start(f32[32,1024]{1,0:T(8,128)S(1)} %shard_map.56), channel_id=1, source_target_pairs={{0,1},{1,0},{2,3},{3,2},{4,5},{5,4},{6,7},{7,6},{8,9},{9,8},{10,11... | collective-permute-start | bytes 393224 | tf_op jit(solution)/shard_map/ppermute | solution.py:204

commit v3 on v1

v3 whole, which is shorter than its diff:
```python
import jax
import jax.numpy as jnp
from jax import lax
from jax.experimental import pallas as pl
from jax.experimental.pallas import tpu as pltpu
from jax.sharding import Mesh, PartitionSpec as P

softness = 0.2
PLANE = ("line", "yl")
TOGETHER = 4


def overload_kernel(where_ref, flow_ref, base_ref, lodf_ref, gain_ref, out_ref, spread, rows, turned, scaled):
    lines, scens = base_ref.shape
    tile = out_ref.shape[1]
    step = pl.program_id(0)

    @pl.when(step == 0)
    def _():
        columns = (base_ref[...] * gain_ref[...]).T
        for line in range(lines):
            spread[line] = jnp.broadcast_to(columns[:, line : line + 1], (scens, 128))

    def fetch(group, carry):
        for offset in range(32):
            slot = group * 32 + offset
            rows[pl.ds(slot, 1), :] = flow_ref[pl.ds(where_ref[step * tile + slot], 1), :]
        return carry

    lax.fori_loop(0, tile // 32, fetch, 0)
    for part in range(tile // 128):
        turned[:, part * 128 : part * 128 + 128] = rows[part * 128 : part * 128 + 128, :].T
    scaled[...] = lodf_ref[...].astype(jnp.float32) * gain_ref[...]

    def some(index, carry):
        first = index * TOGETHER
        factors = []
        for j in range(TOGETHER):
            row = scaled[pl.ds(first + j, 1), :]
            factors.append([jnp.broadcast_to(row[:, k : k + 128], (8, 128)) for k in range(0, tile, 128)])
        sums = [[jnp.zeros((8, 128), jnp.float32) for _ in range(0, tile, 128)] for j in range(TOGETHER)]
        for s in range(0, scens, 8):
            levels = [spread[first + j, s : s + 8, :] for j in range(TOGETHER)]
            for part in range(tile // 128):
                flow = turned[s : s + 8, part * 128 : part * 128 + 128]
                for j in range(TOGETHER):
                    level = levels[j] + factors[j][part] * flow
                    sums[j][part] = sums[j][part] + jnp.tanh(jnp.abs(level) - 0.5 / softness)
        for j in range(TOGETHER):
            out_ref[pl.ds(first + j, 1), :] = jnp.concatenate(
                [jnp.sum(total, axis=0, keepdims=True) for total in sums[j]], axis=1
            )
        return carry

    lax.fori_loop(0, lines // TOGETHER, some, 0)


def overload_sums(where, flow, base, lodf, gain):
    lines, outages = lodf.shape
    scens = base.shape[1]
    tile = min(256, outages)
    return pl.pallas_call(
        overload_kernel,
        out_shape=jax.ShapeDtypeStruct((lines, outages), jnp.float32),
        grid_spec=pltpu.PrefetchScalarGridSpec(
            num_scalar_prefetch=1,
            grid=(outages // tile,),
            in_specs=[
                pl.BlockSpec((outages, scens), lambda i, w: (0, 0), pipeline_mode=pl.Buffered(1)),
                pl.BlockSpec((lines, scens), lambda i, w: (0, 0), pipeline_mode=pl.Buffered(1)),
                pl.BlockSpec((lines, tile), lambda i, w: (0, i)),
                pl.BlockSpec((lines, 1), lambda i, w: (0, 0), pipeline_mode=pl.Buffered(1)),
            ],
            out_specs=pl.BlockSpec((lines, tile), lambda i, w: (0, i)),
            scratch_shapes=[
                pltpu.VMEM((lines, scens, 128), jnp.float32),
                pltpu.VMEM((tile, scens), jnp.float32),
                pltpu.VMEM((scens, tile), jnp.float32),
                pltpu.VMEM((lines, tile), jnp.float32),
            ],
        ),
        compiler_params=pltpu.CompilerParams(vmem_limit_bytes=16 << 20),
        cost_estimate=pl.CostEstimate(
            flops=5 * lines * outages * scens,
            transcendentals=lines * outages * scens,
            bytes_accessed=4 * outages * scens + 6 * lines * outages,
        ),
    )(where, flow, base, lodf, gain)


def exchange(values, axes):
    return lax.all_to_all(values, axes, 0, 0, tiled=True)


def gather_all(rows, axes, members):
    return exchange(jnp.tile(rows, (members, 1)), axes)


def select(choice, values):
    high = lax.reduce_precision(values, 8, 7)
    rest = values - high
    middle = lax.reduce_precision(rest, 8, 7)
    pieces = [piece.astype(jnp.bfloat16) for piece in (high, middle, rest - middle)]
    picked = jnp.dot(
        choice.astype(jnp.bfloat16), jnp.concatenate(pieces, axis=1), preferred_element_type=jnp.float32
    )
    width = values.shape[1]
    return picked[:, :width] + (picked[:, width : 2 * width] + picked[:, 2 * width :])


def halve(rows, axis, bit):
    mine = (lax.axis_index(axis) // bit) % 2
    pairs = [(member, member ^ bit) for member in range(lax.axis_size(axis))]
    sent = lax.dynamic_slice_in_dim(rows, 1 - mine, 1, axis=1)
    return lax.dynamic_slice_in_dim(rows, mine, 1, axis=1) + lax.ppermute(sent, axis, pairs)


def below(outages, limits):
    return jnp.sum((outages[None, :] < limits[:, None]).astype(jnp.int32), axis=1)


def shards(ptdf, injections, lodf, ratings, outages):
    own, count = lodf.shape
    scens = injections.shape[1]
    n_line, n_yl, n_z = (lax.axis_size(name) for name in ("line", "yl", "z"))
    n_class = n_line * n_yl
    line, yl = lax.axis_index("line"), lax.axis_index("yl")
    here = line * n_yl + yl
    group = ptdf.shape[0]
    column = group // n_yl
    depth = count // n_class
    share = -(-group // n_class)

    starts = below(outages, group * jnp.arange(n_line + 1))
    first, number = starts[:-1], starts[1:] - starts[:-1]
    lines = line * group + jnp.arange(group)
    before, through = below(outages, lines), below(outages, lines + 1)
    mine = before - jnp.sum(jnp.where(jnp.arange(n_line) == line, first, 0))
    slot = jnp.where(through > before, (before % n_class) * share + mine // n_class, -1)
    slot, injections = lax.optimization_barrier((slot, injections))

    partial = jnp.dot(ptdf, injections, preferred_element_type=jnp.float32)
    deal = slot[None, :] == jnp.arange(n_class * share)[:, None]
    to_classes = select(deal, partial)
    dealt = exchange(to_classes, PLANE)
    partial, outages, first, number, to_classes = lax.optimization_barrier(
        (partial, outages, first, number, to_classes)
    )
    nth = lax.rem(here - first + count * n_class, n_class)[:, None] + n_class * jnp.arange(share)[None, :]
    row = jnp.where(nth < number[:, None], (first[:, None] + nth) // n_class, -1)
    row = jnp.broadcast_to(row[:, None, :], (n_line, n_yl, share)).reshape(-1)
    collected = select(row[None, :] == jnp.arange(depth)[:, None], dealt)

    base = halve(partial.reshape(1, n_yl, column, scens), "yl", 1)
    base = halve(base.reshape(n_z // 2, 2, own, scens), "z", 1)
    collected, base = lax.optimization_barrier((collected, base))

    class_flow = jnp.sum(exchange(collected, "z").reshape(n_z, -1, scens), axis=0)
    class_flow = gather_all(class_flow, "z", n_z)
    class_flow, base, outages = lax.optimization_barrier((class_flow, base, outages))
    outage_flow = gather_all(class_flow, PLANE, n_class)
    span = 2
    while span < n_z:
        base = halve(base.reshape(n_z // span // 2, 2, own, scens), "z", span)
        span *= 2
    base = base.reshape(own, scens)
    rank = below(outages, outages)
    where = (rank % n_class) * depth + rank // n_class

    gain = (0.5 / (softness * ratings))[:, None]
    local = overload_sums(where, outage_flow, base, lodf, gain)
    total = local + lax.ppermute(local, "scen", [(0, 1), (1, 0)])
    return 0.5 + total * (0.5 / (scens * lax.axis_size("scen")))


def solution(mesh):
    n_line, n_bus, n_scen = (mesh.shape[name] for name in ("line", "bus", "scen"))
    split = Mesh(
        mesh.devices.reshape(n_line, 2, n_bus // 2, n_scen), ("line", "yl", "z", "scen")
    )
    return jax.shard_map(
        shards,
        mesh=split,
        in_specs=(
            P("line", ("yl", "z")),
            P(("yl", "z"), "scen"),
            P(("line", "yl", "z"), None),
            P(("line", "yl", "z")),
            P(),
        ),
        out_specs=P(("line", "yl", "z"), None),
        check_vma=False,
    )
```

time: 183 us -> 179 us (0.978)
  starting transfers between devices: 26.7 us -> 56 us
  blocking collectives: 67.1 us -> 42.4 us
  waiting for transfers between devices: 37.7 us -> 23 us
  other arithmetic: 9.69 us -> 15 us
    all_to_all x2, waiting for transfers between devices: 32.1 us -> 0.01 us  [exchange(): return lax.all_to_all(values, axes, 0, 0, tiled=True)]
    all_to_all x2, blocking collectives: 67.1 us -> 42.4 us  [exchange(): return lax.all_to_all(values, axes, 0, 0, tiled=True)]
    ppermute x1 -> x5, starting transfers between devices: 4.01 us -> 24.6 us  [halve(): lax.ppermute(sent, axis, pairs)]
    ppermute x1 -> x5, waiting for transfers between devices: 4.44 us -> 21.8 us  [halve(): lax.ppermute(sent, axis, pairs)]
    ppermute x1, starting transfers between devices: 6.72 us -> 11.8 us  [shards(): total = local + lax.ppermute(local, 'scen', [(0, 1), (1, 0)])]
    unnamed x13 -> x10, local copies, waits for them, and re-layouts: 4.42 us -> 0.79 us
    all_to_all x2, starting transfers between devices: 15.9 us -> 19.5 us  [exchange(): return lax.all_to_all(values, axes, 0, 0, tiled=True)]
    add x4 -> x8, other arithmetic: 1.36 us -> 4.49 us  [the longest x4 3.28 us: halve(): lax.dynamic_slice_in_dim(rows, mine, 1, axis=1)]
  transfers between devices with their start and end apart: 4 -> 8, of which waited for: 4 -> 6; matrix products, arithmetic and copies ran while one was open for 4% -> 5% of each run, Pallas kernels for 0% -> 0%
where the time goes in v3:
time: 179 us; the launch traced here: 178 us
  starting transfers between devices  56 us (31%)
  blocking collectives  42.4 us (24%)
  Pallas kernels  26.8 us (15%)
  waiting for transfers between devices  23 us (13%)
  other arithmetic  15 us (8%)
  local copies, waits for them, and re-layouts  8.89 us (5%)
  matrix products  5.58 us (3%)
    all_to_all x2, blocking collectives, exchange(): return lax.all_to_all(values, axes, 0, 0, tiled=True)  42.4 us
    pallas_call x1, Pallas kernels, overload_sums(): pl.pallas_call(overload_kernel, out_shape=jax.ShapeDtypeStruct((lines, ou...  26.8 us
    ppermute x5, starting transfers between devices, halve(): lax.ppermute(sent, axis, pairs)  24.6 us
    ppermute x5, waiting for transfers between devices, halve(): lax.ppermute(sent, axis, pairs)  21.8 us
    all_to_all x2, starting transfers between devices, exchange(): return lax.all_to_all(values, axes, 0, 0, tiled=True)  19.5 us
    ppermute x1, starting transfers between devices, shards(): total = local + lax.ppermute(local, 'scen', [(0, 1), (1, 0)])  11.8 us
    reduce_sum x3, other arithmetic, below(): jnp.sum((outages[None, :] < limits[:, None]).astype(jnp.int32), axis=1)  6.29 us
  transfers between devices with their start and end apart: 8, of which 6 were waited for; matrix products, arithmetic and copies ran while one was open for 5% of the time, Pallas kernels for 0%

profile of v3, /device:TPU:1, one launch (start us, length us, event | category | flops | bytes accessed | tf_op | source)
XLA Modules:
  0.0 178.0 jit_solution(6449562393073770574)
XLA Ops:
  0.0 1.0 convert_reduce_fusion.3
  1.7 2.7 %convert_reduce_fusion.2 = (s32[1024]{0:T(1024)S(1)}, s32[1024]{0:T(1024)S(1)}) fusion(s32[2048]{0:T(1024)} %param.9, s32[1024]{0:T(1024)S(1)} %get-tuple-element.40, s32[1024]{0:T(1024)S(1)} %get-tuple-element.39), kind=kLoop, calls=%fused_computation.2 | loop fusion | flops 12580864 | bytes 24576 | tf_op jit(solution)/shard_map/reduce_sum | solution.py:119
  5.1 3.3 %reduce-precision_convert_fusion.3 = (bf16[1024,256]{0,1:T(8,128)(2,1)S(1)}, bf16[1024,256]{0,1:T(8,128)(2,1)S(1)}, bf16[1024,256]{0,1:T(8,128)(2,1)S(1)}, f32[1024,256]{0,1:T(8,128)}) fusion(bf16[1536,256]{1,0:T(8,128)(2,1)} %param.6, bf16[1024,1536]{1,0:T(8,128)(2,1)S(1)} %copy-done), kind=kOutput, calls=%fused_computation.24 | convolution fusion | flops 807141376 | bytes 6553600 | tf_op jit(solution)/shard_map/dot_general | solution.py:142
  8.3 1.9 %fusion = f32[1024,768]{1,0:T(8,128)S(1)} fusion(s32[1024]{0:T(1024)S(1)} %fusion.32, bf16[1024,256]{0,1:T(8,128)(2,1)S(1)} %get-tuple-element.33, bf16[1024,256]{0,1:T(8,128)(2,1)S(1)} %get-tuple-element.34, bf16[1024,256]{0,1:T(8,128)(2,1)S(1)} %get-tuple-element.32), kind=kOutput, calls=%fused_computation.4 | convolution fusion | flops 1616379904 | bytes 4722688 | tf_op jit(solution)/shard_map/dot_general | solution.py:104
  10.3 1.2 fusion.15
  11.4 2.6 %copy.13 = f32[1024,256]{1,0:T(8,128)} copy(f32[1024,256]{0,1:T(8,128)} %get-tuple-element.20) | data formatting | bytes 2097152 | tf_op jit(solution)/shard_map/reshape | solution.py:154
  14.0 1.9 %constant_dynamic-slice_fusion.4 = f32[1,1,512,256]{3,2,1,0:T(8,128)} fusion(f32[1,2,512,256]{3,2,1,0:T(8,128)} %bitcast.23, s32[]{:T(128)S(6)} %select_n.120), kind=kLoop, calls=%fused_computation.87 | loop fusion | bytes 1048580 | tf_op jit(solution)/shard_map/dynamic_slice | solution.py:114
  15.9 4.0 %collective-permute-start = (f32[1,1,512,256]{3,2,1,0:T(8,128)}, f32[1,1,512,256]{3,2,1,0:T(8,128)}, u32[]{:S(2)}, u32[]{:S(2)}) collective-permute-start(f32[1,1,512,256]{3,2,1,0:T(8,128)} %constant_dynamic-slice_fusion.4), channel_id=1, source_target_pairs={{0,32},{32,0},{1,33},{33,1},{2,34},{34,2},{3,35},{35,3},{4,36},{36... | collective-permute-start | bytes 1572872 | tf_op jit(solution)/shard_map/ppermute | solution.py:115
  19.9 6.5 %all-to-all-start = ((f32[16,64,256]{2,1,0:T(8,128)}), f32[16,64,256]{2,1,0:T(8,128)}, u32[]{:S(2)}, u32[]{:S(2)}) async-start(f32[16,64,256]{2,1,0:T(8,128)} %bitcast.25), calls=%async_computation | async-start | bytes 2097152 | tf_op jit(solution)/shard_map/all_to_all | solution.py:92
  27.0 1.3 dynamic-slice_add_fusion
  28.3 0.8 copy-done.2
  29.1 10.0 %collective-permute-start.1 = (f32[8,1,32,256]{3,2,1,0:T(8,128)S(1)}, f32[8,1,32,256]{3,2,1,0:T(8,128)}, u32[]{:S(2)}, u32[]{:S(2)}) collective-permute-start(f32[8,1,32,256]{3,2,1,0:T(8,128)S(1)} %constant_dynamic-slice_fusion.3), channel_id=1, source_target_pairs={{0,2},{2,0},{4,6},{6,4},{8,10},{10,8},{12,14},{14,12},{16,18},{18,... | collective-permute-start | bytes 786440 | tf_op jit(solution)/shard_map/ppermute | solution.py:115
  39.9 3.4 %collective-permute-done.1 = f32[8,1,32,256]{3,2,1,0:T(8,128)} collective-permute-done((f32[8,1,32,256]{3,2,1,0:T(8,128)S(1)}, f32[8,1,32,256]{3,2,1,0:T(8,128)}, u32[]{:S(2)}, u32[]{:S(2)}) %collective-permute-start.1) | collective-permute-done | bytes 262176 | tf_op jit(solution)/shard_map/ppermute | solution.py:115
  43.2 1.1 dynamic-slice_add_fusion.1
  44.3 1.5 reduce-precision_convert_fusion.1
  46.2 26.5 %all_to_all.38 = f32[16,8,256]{2,1,0:T(8,128)S(1)} all-to-all(f32[16,8,256]{2,1,0:T(8,128)S(1)} %bitcast.33), channel_id=1, replica_groups=mesh['line'=8,'yl'=2,'z'=16,'scen'=2] {'z'}, dimensions={0} | all-to-all | bytes 262144 | tf_op jit(solution)/shard_map/all_to_all | solution.py:92
  72.8 15.9 %all_to_all.39 = f32[16,8,256]{2,1,0:T(8,128)S(1)} all-to-all(f32[16,8,256]{2,1,0:T(8,128)S(1)} %tile.4), channel_id=1, replica_groups=mesh['line'=8,'yl'=2,'z'=16,'scen'=2] {'z'}, dimensions={0} | all-to-all | bytes 262144 | tf_op jit(solution)/shard_map/all_to_all | solution.py:92
  88.7 1.5 tile.5
  90.2 13.0 %all-to-all-start.3 = ((f32[16,128,256]{2,1,0:T(8,128)}), f32[16,128,256]{2,1,0:T(8,128)}, u32[]{:S(2)}, u32[]{:S(2)}) async-start(f32[16,128,256]{2,1,0:T(8,128)} %tile.5), calls=%async_computation.3 | async-start | bytes 4194304 | tf_op jit(solution)/shard_map/all_to_all | solution.py:92
  103.9 3.2 %collective-permute-start.2 = (f32[4,1,32,256]{3,2,1,0:T(8,128)}, f32[4,1,32,256]{3,2,1,0:T(8,128)}, u32[]{:S(2)}, u32[]{:S(2)}) collective-permute-start(f32[4,1,32,256]{3,2,1,0:T(8,128)} %constant_dynamic-slice_fusion.2), channel_id=1, source_target_pairs={{0,4},{2,6},{4,0},{6,2},{8,12},{10,14},{12,8},{14,10},{16,20},{18,... | collective-permute-start | bytes 393224 | tf_op jit(solution)/shard_map/ppermute | solution.py:115
  107.7 0.7 copy.12.gain_ref
  108.5 3.8 %collective-permute-done.2 = f32[4,1,32,256]{3,2,1,0:T(8,128)} collective-permute-done((f32[4,1,32,256]{3,2,1,0:T(8,128)}, f32[4,1,32,256]{3,2,1,0:T(8,128)}, u32[]{:S(2)}, u32[]{:S(2)}) %collective-permute-start.2) | collective-permute-done | bytes 131104 | tf_op jit(solution)/shard_map/ppermute | solution.py:115
  112.3 0.9 dynamic-slice_add_fusion.2
  113.2 3.9 %collective-permute-start.3 = (f32[2,1,32,256]{3,2,1,0:T(8,128)S(1)}, f32[2,1,32,256]{3,2,1,0:T(8,128)S(1)}, u32[]{:S(2)}, u32[]{:S(2)}) collective-permute-start(f32[2,1,32,256]{3,2,1,0:T(8,128)S(1)} %constant_dynamic-slice_fusion.1), channel_id=1, source_target_pairs={{0,8},{2,10},{4,12},{6,14},{8,0},{10,2},{12,4},{14,6},{16,24},{18,... | collective-permute-start | bytes 196616 | tf_op jit(solution)/shard_map/ppermute | solution.py:115
  117.1 2.6 %convert_reduce_fusion = s32[2048]{0:T(1024)S(1)} fusion(s32[2048]{0:T(1024)} %param.9), kind=kLoop, calls=%fused_computation | loop fusion | flops 12580864 | bytes 16384 | tf_op jit(solution)/shard_map/reduce_sum | solution.py:119
  119.7 4.3 %collective-permute-done.3 = f32[2,1,32,256]{3,2,1,0:T(8,128)S(1)} collective-permute-done((f32[2,1,32,256]{3,2,1,0:T(8,128)S(1)}, f32[2,1,32,256]{3,2,1,0:T(8,128)S(1)}, u32[]{:S(2)}, u32[]{:S(2)}) %collective-permute-start.3) | collective-permute-done | bytes 65568 | tf_op jit(solution)/shard_map/ppermute | solution.py:115
  124.0 3.6 %collective-permute-start.4 = (f32[1,1,32,256]{3,2,1,0:T(8,128)S(1)}, f32[1,1,32,256]{3,2,1,0:T(8,128)S(1)}, u32[]{:S(2)}, u32[]{:S(2)}) collective-permute-start(f32[1,1,32,256]{3,2,1,0:T(8,128)S(1)} %constant_dynamic-slice_fusion), channel_id=1, source_target_pairs={{0,16},{2,18},{4,20},{6,22},{8,24},{10,26},{12,28},{14,30},{16,0},... | collective-permute-start | bytes 98312 | tf_op jit(solution)/shard_map/ppermute | solution.py:115
  127.6 9.8 %collective-permute-done.4 = f32[1,1,32,256]{3,2,1,0:T(8,128)S(1)} collective-permute-done((f32[1,1,32,256]{3,2,1,0:T(8,128)S(1)}, f32[1,1,32,256]{3,2,1,0:T(8,128)S(1)}, u32[]{:S(2)}, u32[]{:S(2)}) %collective-permute-start.4) | collective-permute-done | bytes 32800 | tf_op jit(solution)/shard_map/ppermute | solution.py:115
  137.4 26.8 %shard_map.55 = f32[32,2048]{1,0:T(8,128)S(1)} custom-call(s32[2048]{0:T(1024)S(1)} %fusion.19.where_ref, f32[2048,256]{1,0:T(8,128)} %bitcast.6.flow_ref, f32[32,256]{1,0:T(8,128)S(1)} %add_bitcast_fusion.base_ref, bf16[32,2048]{1,0:T(8,128)(2,1)S(1)} %copy-done.1, f32[32,1]{1,0:T(8,128)S(1)} %copy.12.gain_ref), custom_call_target="tpu_custom_call" | custom-call | flops 83886080 | bytes 2490368 | tf_op jit(solution)/shard_map/pallas_call | solution.py:62
  164.3 11.8 %collective-permute-start.5 = (f32[32,2048]{1,0:T(8,128)S(1)}, f32[32,2048]{1,0:T(8,128)S(1)}, u32[]{:S(2)}, u32[]{:S(2)}) collective-permute-start(f32[32,2048]{1,0:T(8,128)S(1)} %shard_map.55), channel_id=1, source_target_pairs={{0,1},{1,0},{2,3},{3,2},{4,5},{5,4},{6,7},{7,6},{8,9},{9,8},{10,11... | collective-permute-start | bytes 786440 | tf_op jit(solution)/shard_map/ppermute | solution.py:172
  176.1 1.1 collective-permute-done.5
  177.3 0.7 multiply_add_fusion
  (33 shorter events, 4.4 us)
Async XLA Ops:
  0.0 5.0 %copy-start = (bf16[1024,1536]{1,0:T(8,128)(2,1)S(1)}, bf16[1024,1536]{1,0:T(8,128)(2,1)}, u32[]{:S(2)}) copy-start(bf16[1024,1536]{1,0:T(8,128)(2,1)} %param.5) | copy-start | bytes 9437188
  15.9 11.1 %collective-permute-start = (f32[1,1,512,256]{3,2,1,0:T(8,128)}, f32[1,1,512,256]{3,2,1,0:T(8,128)}, u32[]{:S(2)}, u32[]{:S(2)}) collective-permute-start(f32[1,1,512,256]{3,2,1,0:T(8,128)} %constant_dynamic-slice_fusion.4), channel_id=1, source_target_pairs={{0,32},{32,0},{1,33},{33,1},{2,34},{34,2},{3,35},{35,3},{4,36},{36... | collective-permute-start | bytes 1572872 | tf_op jit(solution)/shard_map/ppermute | solution.py:115
  19.9 24.4 %all-to-all-start = ((f32[16,64,256]{2,1,0:T(8,128)}), f32[16,64,256]{2,1,0:T(8,128)}, u32[]{:S(2)}, u32[]{:S(2)}) async-start(f32[16,64,256]{2,1,0:T(8,128)} %bitcast.25), calls=%async_computation | async-start | bytes 2097152 | tf_op jit(solution)/shard_map/all_to_all | solution.py:92
  28.3 0.8 copy-start.2
  29.1 14.2 %collective-permute-start.1 = (f32[8,1,32,256]{3,2,1,0:T(8,128)S(1)}, f32[8,1,32,256]{3,2,1,0:T(8,128)}, u32[]{:S(2)}, u32[]{:S(2)}) collective-permute-start(f32[8,1,32,256]{3,2,1,0:T(8,128)S(1)} %constant_dynamic-slice_fusion.3), channel_id=1, source_target_pairs={{0,2},{2,0},{4,6},{6,4},{8,10},{10,8},{12,14},{14,12},{16,18},{18,... | collective-permute-start | bytes 786440 | tf_op jit(solution)/shard_map/ppermute | solution.py:115
  43.2 2.6 %copy-start.3 = (s32[1024]{0:T(1024)S(1)}, s32[1024]{0:T(1024)}, u32[]{:S(2)}) copy-start(s32[1024]{0:T(1024)} %eq.49) | copy-start | bytes 12292
  88.7 18.5 %copy-start.4 = (f32[32]{0:T(128)S(1)}, f32[32]{0:T(128)}, u32[]{:S(2)}) copy-start(f32[32]{0:T(128)} %param.8) | copy-start | bytes 388
  90.2 47.3 %copy-start.1 = (bf16[32,2048]{1,0:T(8,128)(2,1)S(1)}, bf16[32,2048]{1,0:T(8,128)(2,1)}, u32[]{:S(2)}) copy-start(bf16[32,2048]{1,0:T(8,128)(2,1)} %lodf_ref.1) | copy-start | bytes 393220
  90.2 47.2 %all-to-all-start.3 = ((f32[16,128,256]{2,1,0:T(8,128)}), f32[16,128,256]{2,1,0:T(8,128)}, u32[]{:S(2)}, u32[]{:S(2)}) async-start(f32[16,128,256]{2,1,0:T(8,128)} %tile.5), calls=%async_computation.3 | async-start | bytes 4194304 | tf_op jit(solution)/shard_map/all_to_all | solution.py:92
  103.9 8.3 %collective-permute-start.2 = (f32[4,1,32,256]{3,2,1,0:T(8,128)}, f32[4,1,32,256]{3,2,1,0:T(8,128)}, u32[]{:S(2)}, u32[]{:S(2)}) collective-permute-start(f32[4,1,32,256]{3,2,1,0:T(8,128)} %constant_dynamic-slice_fusion.2), channel_id=1, source_target_pairs={{0,4},{2,6},{4,0},{6,2},{8,12},{10,14},{12,8},{14,10},{16,20},{18,... | collective-permute-start | bytes 393224 | tf_op jit(solution)/shard_map/ppermute | solution.py:115
  113.2 10.8 %collective-permute-start.3 = (f32[2,1,32,256]{3,2,1,0:T(8,128)S(1)}, f32[2,1,32,256]{3,2,1,0:T(8,128)S(1)}, u32[]{:S(2)}, u32[]{:S(2)}) collective-permute-start(f32[2,1,32,256]{3,2,1,0:T(8,128)S(1)} %constant_dynamic-slice_fusion.1), channel_id=1, source_target_pairs={{0,8},{2,10},{4,12},{6,14},{8,0},{10,2},{12,4},{14,6},{16,24},{18,... | collective-permute-start | bytes 196616 | tf_op jit(solution)/shard_map/ppermute | solution.py:115
  124.0 13.4 %collective-permute-start.4 = (f32[1,1,32,256]{3,2,1,0:T(8,128)S(1)}, f32[1,1,32,256]{3,2,1,0:T(8,128)S(1)}, u32[]{:S(2)}, u32[]{:S(2)}) collective-permute-start(f32[1,1,32,256]{3,2,1,0:T(8,128)S(1)} %constant_dynamic-slice_fusion), channel_id=1, source_target_pairs={{0,16},{2,18},{4,20},{6,22},{8,24},{10,26},{12,28},{14,30},{16,0},... | collective-permute-start | bytes 98312 | tf_op jit(solution)/shard_map/ppermute | solution.py:115
  164.3 13.0 %collective-permute-start.5 = (f32[32,2048]{1,0:T(8,128)S(1)}, f32[32,2048]{1,0:T(8,128)S(1)}, u32[]{:S(2)}, u32[]{:S(2)}) collective-permute-start(f32[32,2048]{1,0:T(8,128)S(1)} %shard_map.55), channel_id=1, source_target_pairs={{0,1},{1,0},{2,3},{3,2},{4,5},{5,4},{6,7},{7,6},{8,9},{9,8},{10,11... | collective-permute-start | bytes 786440 | tf_op jit(solution)/shard_map/ppermute | solution.py:172

commit v4 on v3

--- a/solution.py
+++ b/solution.py
@@ -3,6 +3,7 @@
 from jax import lax
 from jax.experimental import pallas as pl
 from jax.experimental.pallas import tpu as pltpu
+from jax.experimental.layout import Layout, with_layout_constraint
 from jax.sharding import Mesh, PartitionSpec as P
 
 softness = 0.2
@@ -108,6 +109,13 @@
     return picked[:, :width] + (picked[:, width : 2 * width] + picked[:, 2 * width :])
 
 
+def carry_over_z(rows, others):
+    members, height, scens = rows.shape
+    both = jnp.concatenate([rows, others], axis=1)
+    both = exchange(both.reshape(-1, scens), "z").reshape(both.shape)
+    return both[:, :height], both[:, height:]
+
+
 def halve(rows, axis, bit):
     mine = (lax.axis_index(axis) // bit) % 2
     pairs = [(member, member ^ bit) for member in range(lax.axis_size(axis))]
@@ -140,6 +148,7 @@
     slot, injections = lax.optimization_barrier((slot, injections))
 
     partial = jnp.dot(ptdf, injections, preferred_element_type=jnp.float32)
+    partial = with_layout_constraint(partial, Layout((0, 1)))
     deal = slot[None, :] == jnp.arange(n_class * share)[:, None]
     to_classes = select(deal, partial)
     dealt = exchange(to_classes, PLANE)
@@ -151,19 +160,19 @@
     row = jnp.broadcast_to(row[:, None, :], (n_line, n_yl, share)).reshape(-1)
     collected = select(row[None, :] == jnp.arange(depth)[:, None], dealt)
 
-    base = halve(partial.reshape(1, n_yl, column, scens), "yl", 1)
-    base = halve(base.reshape(n_z // 2, 2, own, scens), "z", 1)
+    base = halve(partial.reshape(1, n_yl, column, scens), "yl", 1).reshape(n_z, own, scens)
+    collected = collected.reshape(n_z, depth // n_z, scens)
     collected, base = lax.optimization_barrier((collected, base))
 
-    class_flow = jnp.sum(exchange(collected, "z").reshape(n_z, -1, scens), axis=0)
-    class_flow = gather_all(class_flow, "z", n_z)
-    class_flow, base, outages = lax.optimization_barrier((class_flow, base, outages))
+    class_flow, base_first = carry_over_z(collected, base[:, : own // 2])
+    class_flow, base_first = lax.optimization_barrier((jnp.sum(class_flow, axis=0), jnp.sum(base_first, axis=0)))
+    class_flow = jnp.broadcast_to(class_flow, collected.shape)
+    class_flow, base_second = carry_over_z(class_flow, base[:, own // 2 :])
+    class_flow, base_second, outages = lax.optimization_barrier(
+        (class_flow.reshape(depth, scens), jnp.sum(base_second, axis=0), outages)
+    )
     outage_flow = gather_all(class_flow, PLANE, n_class)
-    span = 2
-    while span < n_z:
-        base = halve(base.reshape(n_z // span // 2, 2, own, scens), "z", span)
-        span *= 2
-    base = base.reshape(own, scens)
+    base = jnp.concatenate([base_first, base_second])
     rank = below(outages, outages)
     where = (rank % n_class) * depth + rank // n_class
 

time: 179 us -> 183 us (1.022)
  the two profiles are of different devices: /device:TPU:1 before, /device:TPU:33 now
where the time goes in v4:
time: 183 us; the launch traced here: 182 us
  blocking collectives  64.8 us (35%)
  waiting for transfers between devices  45.5 us (25%)
  Pallas kernels  26.8 us (15%)
  starting transfers between devices  22.6 us (12%)
  other arithmetic  12.6 us (7%)
  matrix products  5.43 us (3%)
  local copies, waits for them, and re-layouts  4.24 us (2%)
    all_to_all x2, blocking collectives, exchange(): return lax.all_to_all(values, axes, 0, 0, tiled=True)  64.8 us
    pallas_call x1, Pallas kernels, overload_sums(): pl.pallas_call(overload_kernel, out_shape=jax.ShapeDtypeStruct((lines, ou...  26.8 us
    all_to_all x2, waiting for transfers between devices, exchange(): return lax.all_to_all(values, axes, 0, 0, tiled=True)  24.7 us
    ppermute x1, waiting for transfers between devices, halve(): lax.ppermute(sent, axis, pairs)  19.7 us
    all_to_all x2, starting transfers between devices, exchange(): return lax.all_to_all(values, axes, 0, 0, tiled=True)  12.6 us
    ppermute x1, starting transfers between devices, shards(): total = local + lax.ppermute(local, 'scen', [(0, 1), (1, 0)])  6.75 us
    reduce_sum x3, other arithmetic, below(): jnp.sum((outages[None, :] < limits[:, None]).astype(jnp.int32), axis=1)  5.51 us
  transfers between devices with their start and end apart: 4, of which 3 were waited for; matrix products, arithmetic and copies ran while one was open for 3% of the time, Pallas kernels for 0%

profile of v4, /device:TPU:33, one launch (start us, length us, event | category | flops | bytes accessed | tf_op | source)
XLA Modules:
  0.0 182.2 jit_solution(10624242883194636216)
XLA Ops:
  0.0 1.0 convert_reduce_fusion.3
  1.1 0.6 slice_subtract_fusion
  1.7 2.7 %convert_reduce_fusion.2 = (s32[1024]{0:T(1024)S(1)}, s32[1024]{0:T(1024)S(1)}) fusion(s32[2048]{0:T(1024)} %param.9, s32[1024]{0:T(1024)S(1)} %get-tuple-element.46, s32[1024]{0:T(1024)S(1)} %get-tuple-element.45), kind=kLoop, calls=%fused_computation.2 | loop fusion | flops 12580864 | bytes 24576 | tf_op jit(solution)/shard_map/reduce_sum | solution.py:127
  4.4 0.7 fusion.33
  5.1 3.1 %reduce-precision_convert_fusion.3 = (bf16[1024,256]{1,0:T(8,128)(2,1)S(1)}, bf16[1024,256]{1,0:T(8,128)(2,1)S(1)}, bf16[1024,256]{1,0:T(8,128)(2,1)S(1)}, f32[1024,256]{1,0:T(8,128)}) fusion(bf16[1024,1536]{1,0:T(8,128)(2,1)S(1)} %copy-done, bf16[1536,256]{1,0:T(8,128)(2,1)} %param.6), kind=kOutput, calls=%fused_computation.24 | convolution fusion | flops 807141376 | bytes 6553600 | tf_op jit(solution)/shard_map/dot_general | solution.py:150
  8.2 1.9 %fusion = f32[1024,768]{1,0:T(8,128)S(1)} fusion(s32[1024]{0:T(1024)S(1)} %fusion.33, bf16[1024,256]{1,0:T(8,128)(2,1)S(1)} %get-tuple-element.37, bf16[1024,256]{1,0:T(8,128)(2,1)S(1)} %get-tuple-element.38, bf16[1024,256]{1,0:T(8,128)(2,1)S(1)} %get-tuple-element.36), kind=kOutput, calls=%fused_computation.4 | convolution fusion | flops 1616379904 | bytes 4722688 | tf_op jit(solution)/shard_map/dot_general | solution.py:105
  10.1 1.2 fusion.15
  11.3 6.8 %all-to-all-start = ((f32[16,64,256]{2,1,0:T(8,128)}), f32[16,64,256]{2,1,0:T(8,128)}, u32[]{:S(2)}, u32[]{:S(2)}) async-start(f32[16,64,256]{2,1,0:T(8,128)} %bitcast.21), calls=%async_computation | async-start | bytes 2097152 | tf_op jit(solution)/shard_map/all_to_all | solution.py:93
  18.2 1.9 %constant_dynamic-slice_fusion = f32[1,1,512,256]{3,2,1,0:T(8,128)} fusion(f32[1,2,512,256]{3,2,1,0:T(8,128)} %bitcast.23, s32[]{:T(128)S(6)} %select_n.70), kind=kLoop, calls=%fused_computation.97 | loop fusion | bytes 1048580 | tf_op jit(solution)/shard_map/dynamic_slice | solution.py:122
  20.0 3.2 %collective-permute-start = (f32[1,1,512,256]{3,2,1,0:T(8,128)}, f32[1,1,512,256]{3,2,1,0:T(8,128)}, u32[]{:S(2)}, u32[]{:S(2)}) collective-permute-start(f32[1,1,512,256]{3,2,1,0:T(8,128)} %constant_dynamic-slice_fusion), channel_id=1, source_target_pairs={{0,32},{32,0},{1,33},{33,1},{2,34},{34,2},{3,35},{35,3},{4,36},{36... | collective-permute-start | bytes 1572872 | tf_op jit(solution)/shard_map/ppermute | solution.py:123
  23.3 0.1 fusion.36
  23.4 0.1 eq.45
  23.5 19.7 %collective-permute-done = f32[1,1,512,256]{3,2,1,0:T(8,128)} collective-permute-done((f32[1,1,512,256]{3,2,1,0:T(8,128)}, f32[1,1,512,256]{3,2,1,0:T(8,128)}, u32[]{:S(2)}, u32[]{:S(2)}) %collective-permute-start) | collective-permute-done | bytes 524320 | tf_op jit(solution)/shard_map/ppermute | solution.py:123
  43.1 2.1 %dynamic-slice_add_fusion = f32[1,1,512,256]{3,2,1,0:T(8,128)} fusion(f32[1,1,512,256]{3,2,1,0:T(8,128)} %collective-permute-done, f32[1,2,512,256]{3,2,1,0:T(8,128)} %bitcast.24, s32[]{:T(128)S(6)} %select_n.69), kind=kLoop, calls=%fused_computation.30 | loop fusion | flops 131072 | bytes 1572868 | tf_op jit(solution)/shard_map/add | solution.py:123
  45.2 0.0 all-to-all-done
  45.2 1.5 reduce-precision_convert_fusion.1
  46.7 0.4 fusion.7
  47.1 0.6 copy-done.2
  47.8 35.5 %all_to_all.32 = f32[16,24,256]{2,1,0:T(8,128)S(1)} all-to-all(f32[16,24,256]{2,1,0:T(8,128)S(1)} %pad_maximum_fusion), channel_id=1, replica_groups=mesh['line'=8,'yl'=2,'z'=16,'scen'=2] {'z'}, dimensions={0} | all-to-all | bytes 786432 | tf_op jit(solution)/shard_map/all_to_all | solution.py:93
  83.4 29.3 %all_to_all.33 = f32[16,24,256]{2,1,0:T(8,128)S(1)} all-to-all(f32[16,24,256]{2,1,0:T(8,128)S(1)} %pad_maximum_fusion.1), channel_id=1, replica_groups=mesh['line'=8,'yl'=2,'z'=16,'scen'=2] {'z'}, dimensions={0} | all-to-all | bytes 786432 | tf_op jit(solution)/shard_map/all_to_all | solution.py:93
  112.8 0.0 copy-start.4
  112.8 0.0 copy-start.3
  112.8 0.0 copy-start.1
  112.8 1.5 tile.2
  114.3 5.8 %all-to-all-start.3 = ((f32[16,128,256]{2,1,0:T(8,128)}), f32[16,128,256]{2,1,0:T(8,128)}, u32[]{:S(2)}, u32[]{:S(2)}) async-start(f32[16,128,256]{2,1,0:T(8,128)} %tile.2), calls=%async_computation.3 | async-start | bytes 4194304 | tf_op jit(solution)/shard_map/all_to_all | solution.py:93
  120.2 0.1 copy.7.gain_ref
  120.3 1.8 convert_reduce_fusion
  122.1 24.7 %all-to-all-done.3 = f32[16,128,256]{2,1,0:T(8,128)} async-done(((f32[16,128,256]{2,1,0:T(8,128)}), f32[16,128,256]{2,1,0:T(8,128)}, u32[]{:S(2)}, u32[]{:S(2)}) %all-to-all-start.3) | async-done | bytes 2097184 | tf_op jit(solution)/shard_map/all_to_all | solution.py:93
  146.8 26.8 %shard_map.55 = f32[32,2048]{1,0:T(8,128)S(1)} custom-call(s32[2048]{0:T(1024)S(1)} %fusion.20.where_ref, f32[2048,256]{1,0:T(8,128)} %bitcast.7.flow_ref, f32[32,256]{1,0:T(8,128)S(1)} %pad_maximum_fusion.2.base_ref, bf16[32,2048]{1,0:T(8,128)(2,1)S(1)} %copy-done.1, f32[32,1]{1,0:T(8,128)S(1)} %copy.7.gain_ref), custom_call_target="tpu_custom_call" | custom-call | flops 83886080 | bytes 2490368 | tf_op jit(solution)/shard_map/pallas_call | solution.py:63
  173.6 6.7 %collective-permute-start.1 = (f32[32,2048]{1,0:T(8,128)S(1)}, f32[32,2048]{1,0:T(8,128)S(1)}, u32[]{:S(2)}, u32[]{:S(2)}) collective-permute-start(f32[32,2048]{1,0:T(8,128)S(1)} %shard_map.55), channel_id=1, source_target_pairs={{0,1},{1,0},{2,3},{3,2},{4,5},{5,4},{6,7},{7,6},{8,9},{9,8},{10,11... | collective-permute-start | bytes 786440 | tf_op jit(solution)/shard_map/ppermute | solution.py:181
  180.4 1.1 collective-permute-done.1
  181.5 0.7 multiply_add_fusion
  (23 shorter events, 0.3 us)
Async XLA Ops:
  0.0 5.0 %copy-start = (bf16[1024,1536]{1,0:T(8,128)(2,1)S(1)}, bf16[1024,1536]{1,0:T(8,128)(2,1)}, u32[]{:S(2)}) copy-start(bf16[1024,1536]{1,0:T(8,128)(2,1)} %param.5) | copy-start | bytes 9437188
  11.3 33.9 %all-to-all-start = ((f32[16,64,256]{2,1,0:T(8,128)}), f32[16,64,256]{2,1,0:T(8,128)}, u32[]{:S(2)}, u32[]{:S(2)}) async-start(f32[16,64,256]{2,1,0:T(8,128)} %bitcast.21), calls=%async_computation | async-start | bytes 2097152 | tf_op jit(solution)/shard_map/all_to_all | solution.py:93
  20.0 23.1 %collective-permute-start = (f32[1,1,512,256]{3,2,1,0:T(8,128)}, f32[1,1,512,256]{3,2,1,0:T(8,128)}, u32[]{:S(2)}, u32[]{:S(2)}) collective-permute-start(f32[1,1,512,256]{3,2,1,0:T(8,128)} %constant_dynamic-slice_fusion), channel_id=1, source_target_pairs={{0,32},{32,0},{1,33},{33,1},{2,34},{34,2},{3,35},{35,3},{4,36},{36... | collective-permute-start | bytes 1572872 | tf_op jit(solution)/shard_map/ppermute | solution.py:123
  46.7 1.0 copy-start.2
  112.8 7.4 %copy-start.4 = (f32[32]{0:T(128)S(1)}, f32[32]{0:T(128)}, u32[]{:S(2)}) copy-start(f32[32]{0:T(128)} %param.8) | copy-start | bytes 388
  112.8 7.5 %copy-start.3 = (s32[2048]{0:T(1024)S(1)}, s32[2048]{0:T(1024)}, u32[]{:S(2)}) copy-start(s32[2048]{0:T(1024)} %param.9) | copy-start | bytes 24580
  112.8 34.0 %copy-start.1 = (bf16[32,2048]{1,0:T(8,128)(2,1)S(1)}, bf16[32,2048]{1,0:T(8,128)(2,1)}, u32[]{:S(2)}) copy-start(bf16[32,2048]{1,0:T(8,128)(2,1)} %lodf_ref.1) | copy-start | bytes 393220
  114.3 32.5 %all-to-all-start.3 = ((f32[16,128,256]{2,1,0:T(8,128)}), f32[16,128,256]{2,1,0:T(8,128)}, u32[]{:S(2)}, u32[]{:S(2)}) async-start(f32[16,128,256]{2,1,0:T(8,128)} %tile.2), calls=%async_computation.3 | async-start | bytes 4194304 | tf_op jit(solution)/shard_map/all_to_all | solution.py:93
  173.6 7.9 %collective-permute-start.1 = (f32[32,2048]{1,0:T(8,128)S(1)}, f32[32,2048]{1,0:T(8,128)S(1)}, u32[]{:S(2)}, u32[]{:S(2)}) collective-permute-start(f32[32,2048]{1,0:T(8,128)S(1)} %shard_map.55), channel_id=1, source_target_pairs={{0,1},{1,0},{2,3},{3,2},{4,5},{5,4},{6,7},{7,6},{8,9},{9,8},{10,11... | collective-permute-start | bytes 786440 | tf_op jit(solution)/shard_map/ppermute | solution.py:181

commit v5 on v3

--- a/solution.py
+++ b/solution.py
@@ -3,6 +3,7 @@
 from jax import lax
 from jax.experimental import pallas as pl
 from jax.experimental.pallas import tpu as pltpu
+from jax.experimental.layout import Layout, with_layout_constraint
 from jax.sharding import Mesh, PartitionSpec as P
 
 softness = 0.2
@@ -38,7 +39,7 @@
         for j in range(TOGETHER):
             row = scaled[pl.ds(first + j, 1), :]
             factors.append([jnp.broadcast_to(row[:, k : k + 128], (8, 128)) for k in range(0, tile, 128)])
-        sums = [[jnp.zeros((8, 128), jnp.float32) for _ in range(0, tile, 128)] for j in range(TOGETHER)]
+        sums = [[jnp.zeros((8, 128), jnp.float32) for _ in range(0, tile, 128)] for _ in range(TOGETHER)]
         for s in range(0, scens, 8):
             levels = [spread[first + j, s : s + 8, :] for j in range(TOGETHER)]
             for part in range(tile // 128):
@@ -119,7 +120,7 @@
     return jnp.sum((outages[None, :] < limits[:, None]).astype(jnp.int32), axis=1)
 
 
-def shards(ptdf, injections, lodf, ratings, outages):
+def screen(ptdf, injections, lodf, ratings, outages):
     own, count = lodf.shape
     scens = injections.shape[1]
     n_line, n_yl, n_z = (lax.axis_size(name) for name in ("line", "yl", "z"))
@@ -140,6 +141,7 @@
     slot, injections = lax.optimization_barrier((slot, injections))
 
     partial = jnp.dot(ptdf, injections, preferred_element_type=jnp.float32)
+    partial = with_layout_constraint(partial, Layout((0, 1)))
     deal = slot[None, :] == jnp.arange(n_class * share)[:, None]
     to_classes = select(deal, partial)
     dealt = exchange(to_classes, PLANE)
@@ -152,14 +154,22 @@
     collected = select(row[None, :] == jnp.arange(depth)[:, None], dealt)
 
     base = halve(partial.reshape(1, n_yl, column, scens), "yl", 1)
+    collected, base = lax.optimization_barrier((collected, base))
+
     base = halve(base.reshape(n_z // 2, 2, own, scens), "z", 1)
-    collected, base = lax.optimization_barrier((collected, base))
-
-    class_flow = jnp.sum(exchange(collected, "z").reshape(n_z, -1, scens), axis=0)
+    class_flow = exchange(collected, "z")
+    class_flow = jnp.sum(class_flow.reshape(n_z, -1, scens), axis=0)
+    class_flow, base = lax.optimization_barrier((class_flow, base))
+    span = 2
+    if span < n_z:
+        base = halve(base.reshape(n_z // span // 2, 2, own, scens), "z", span)
+        span *= 2
     class_flow = gather_all(class_flow, "z", n_z)
     class_flow, base, outages = lax.optimization_barrier((class_flow, base, outages))
+    if span < n_z:
+        base = halve(base.reshape(n_z // span // 2, 2, own, scens), "z", span)
+        span *= 2
     outage_flow = gather_all(class_flow, PLANE, n_class)
-    span = 2
     while span < n_z:
         base = halve(base.reshape(n_z // span // 2, 2, own, scens), "z", span)
         span *= 2
@@ -179,7 +189,7 @@
         mesh.devices.reshape(n_line, 2, n_bus // 2, n_scen), ("line", "yl", "z", "scen")
     )
     return jax.shard_map(
-        shards,
+        screen,
         mesh=split,
         in_specs=(
             P("line", ("yl", "z")),

time: 179 us -> 171 us (0.955)
  blocking collectives: 42.4 us -> 0 us
  waiting for transfers between devices: 23 us -> 49.9 us
  starting transfers between devices: 56 us -> 67.2 us
  local copies, waits for them, and re-layouts: 8.89 us -> 4.95 us
    all_to_all x2 -> x0, blocking collectives: 42.4 us -> none  [exchange(): return lax.all_to_all(values, axes, 0, 0, tiled=True)]
    ppermute x5, waiting for transfers between devices: 21.8 us -> 37.6 us  [halve(): lax.ppermute(sent, axis, pairs)]
    all_to_all x2 -> x4, starting transfers between devices: 19.5 us -> 33.1 us  [exchange(): return lax.all_to_all(values, axes, 0, 0, tiled=True)]
    all_to_all x2 -> x4, waiting for transfers between devices: 0.01 us -> 11.2 us  [exchange(): return lax.all_to_all(values, axes, 0, 0, tiled=True)]
    ppermute x1, starting transfers between devices: 11.8 us -> 7.01 us  [screen(): total = local + lax.ppermute(local, 'scen', [(0, 1), (1, 0)])]
    reshape x1 -> x0, local copies, waits for them, and re-layouts: 2.56 us -> none  [shards(): base = halve(partial.reshape(1, n_yl, column, scens), 'yl', 1)]
    ppermute x5, starting transfers between devices: 24.6 us -> 27.1 us  [halve(): lax.ppermute(sent, axis, pairs)]
  transfers between devices with their start and end apart: 8 -> 10, of which waited for: 6 -> 7; matrix products, arithmetic and copies ran while one was open for 5% -> 5% of each run, Pallas kernels for 0% -> 0%
where the time goes in v5:
time: 171 us
  starting transfers between devices  67.2 us (39%)
  waiting for transfers between devices  49.9 us (29%)
  Pallas kernels  26.8 us (16%)
  other arithmetic  15.8 us (9%)
  matrix products  5.43 us (3%)
  local copies, waits for them, and re-layouts  4.95 us (3%)
    ppermute x5, waiting for transfers between devices, halve(): lax.ppermute(sent, axis, pairs)  37.6 us
    all_to_all x4, starting transfers between devices, exchange(): return lax.all_to_all(values, axes, 0, 0, tiled=True)  33.1 us
    ppermute x5, starting transfers between devices, halve(): lax.ppermute(sent, axis, pairs)  27.1 us
    pallas_call x1, Pallas kernels, overload_sums(): pl.pallas_call(overload_kernel, out_shape=jax.ShapeDtypeStruct((lines, ou...  26.8 us
    all_to_all x4, waiting for transfers between devices, exchange(): return lax.all_to_all(values, axes, 0, 0, tiled=True)  11.2 us
    ppermute x1, starting transfers between devices, screen(): total = local + lax.ppermute(local, 'scen', [(0, 1), (1, 0)])  7.01 us
    reduce_sum x3, other arithmetic, below(): jnp.sum((outages[None, :] < limits[:, None]).astype(jnp.int32), axis=1)  5.51 us
    add x4, other arithmetic, halve(): lax.dynamic_slice_in_dim(rows, mine, 1, axis=1)  4.69 us
  transfers between devices with their start and end apart: 10, of which 7 were waited for; matrix products, arithmetic and copies ran while one was open for 5% of the time, Pallas kernels for 0%

profile of v5, /device:TPU:1, one launch (start us, length us, event | category | flops | bytes accessed | tf_op | source)
XLA Modules:
  0.0 170.5 jit_solution(3327894065008432266)
XLA Ops:
  0.0 1.0 convert_reduce_fusion.3
  1.7 2.7 %convert_reduce_fusion.2 = (s32[1024]{0:T(1024)S(1)}, s32[1024]{0:T(1024)S(1)}) fusion(s32[2048]{0:T(1024)} %param.9, s32[1024]{0:T(1024)S(1)} %get-tuple-element.44, s32[1024]{0:T(1024)S(1)} %get-tuple-element.43), kind=kLoop, calls=%fused_computation.2 | loop fusion | flops 12580864 | bytes 24576 | tf_op jit(solution)/shard_map/reduce_sum | solution.py:120
  5.1 3.1 %reduce-precision_convert_fusion.3 = (bf16[1024,256]{1,0:T(8,128)(2,1)S(1)}, bf16[1024,256]{1,0:T(8,128)(2,1)S(1)}, bf16[1024,256]{1,0:T(8,128)(2,1)S(1)}, f32[1024,256]{1,0:T(8,128)}) fusion(bf16[1024,1536]{1,0:T(8,128)(2,1)S(1)} %copy-done, bf16[1536,256]{1,0:T(8,128)(2,1)} %param.6), kind=kOutput, calls=%fused_computation.24 | convolution fusion | flops 807141376 | bytes 6553600 | tf_op jit(solution)/shard_map/dot_general | solution.py:143
  8.2 1.9 %fusion = f32[1024,768]{1,0:T(8,128)S(1)} fusion(s32[1024]{0:T(1024)S(1)} %fusion.32, bf16[1024,256]{1,0:T(8,128)(2,1)S(1)} %get-tuple-element.37, bf16[1024,256]{1,0:T(8,128)(2,1)S(1)} %get-tuple-element.38, bf16[1024,256]{1,0:T(8,128)(2,1)S(1)} %get-tuple-element.36), kind=kOutput, calls=%fused_computation.4 | convolution fusion | flops 1616379904 | bytes 4722688 | tf_op jit(solution)/shard_map/dot_general | solution.py:105
  10.1 1.2 fusion.15
  11.3 7.6 %all-to-all-start = ((f32[16,64,256]{2,1,0:T(8,128)}), f32[16,64,256]{2,1,0:T(8,128)}, u32[]{:S(2)}, u32[]{:S(2)}) async-start(f32[16,64,256]{2,1,0:T(8,128)} %bitcast.23), calls=%async_computation | async-start | bytes 2097152 | tf_op jit(solution)/shard_map/all_to_all | solution.py:93
  19.0 1.9 %constant_dynamic-slice_fusion.4 = f32[1,1,512,256]{3,2,1,0:T(8,128)} fusion(f32[1,2,512,256]{3,2,1,0:T(8,128)} %bitcast.26, s32[]{:T(128)S(6)} %select_n.120), kind=kLoop, calls=%fused_computation.87 | loop fusion | bytes 1048580 | tf_op jit(solution)/shard_map/dynamic_slice | solution.py:115
  20.9 3.2 %collective-permute-start = (f32[1,1,512,256]{3,2,1,0:T(8,128)}, f32[1,1,512,256]{3,2,1,0:T(8,128)}, u32[]{:S(2)}, u32[]{:S(2)}) collective-permute-start(f32[1,1,512,256]{3,2,1,0:T(8,128)} %constant_dynamic-slice_fusion.4), channel_id=1, source_target_pairs={{0,32},{32,0},{1,33},{33,1},{2,34},{34,2},{3,35},{35,3},{4,36},{36... | collective-permute-start | bytes 1572872 | tf_op jit(solution)/shard_map/ppermute | solution.py:116
  24.3 19.7 %collective-permute-done = f32[1,1,512,256]{3,2,1,0:T(8,128)} collective-permute-done((f32[1,1,512,256]{3,2,1,0:T(8,128)}, f32[1,1,512,256]{3,2,1,0:T(8,128)}, u32[]{:S(2)}, u32[]{:S(2)}) %collective-permute-start) | collective-permute-done | bytes 524320 | tf_op jit(solution)/shard_map/ppermute | solution.py:116
  44.0 2.1 %dynamic-slice_add_fusion = f32[1,1,512,256]{3,2,1,0:T(8,128)} fusion(f32[1,1,512,256]{3,2,1,0:T(8,128)} %collective-permute-done, f32[1,2,512,256]{3,2,1,0:T(8,128)} %bitcast.27, s32[]{:T(128)S(6)} %select_n.119), kind=kLoop, calls=%fused_computation.30 | loop fusion | flops 131072 | bytes 1572868 | tf_op jit(solution)/shard_map/add | solution.py:116
  46.1 1.5 reduce-precision_convert_fusion.1
  47.9 0.7 fusion.17
  48.6 3.5 %collective-permute-start.1 = (f32[8,1,32,256]{3,2,1,0:T(8,128)S(1)}, f32[8,1,32,256]{3,2,1,0:T(8,128)}, u32[]{:S(2)}, u32[]{:S(2)}) collective-permute-start(f32[8,1,32,256]{3,2,1,0:T(8,128)S(1)} %constant_dynamic-slice_fusion.3), channel_id=1, source_target_pairs={{0,2},{2,0},{4,6},{6,4},{8,10},{10,8},{12,14},{14,12},{16,18},{18,... | collective-permute-start | bytes 786440 | tf_op jit(solution)/shard_map/ppermute | solution.py:116
  52.1 14.0 %all-to-all-start.1 = ((f32[16,8,256]{2,1,0:T(8,128)}), f32[16,8,256]{2,1,0:T(8,128)S(1)}, u32[]{:S(2)}, u32[]{:S(2)}) async-start(f32[16,8,256]{2,1,0:T(8,128)} %bitcast.4), calls=%async_computation.1 | async-start | bytes 262144 | tf_op jit(solution)/shard_map/all_to_all | solution.py:93
  66.2 1.1 dynamic-slice_add_fusion.1
  67.3 10.9 %all-to-all-done.1 = f32[16,8,256]{2,1,0:T(8,128)S(1)} async-done(((f32[16,8,256]{2,1,0:T(8,128)}), f32[16,8,256]{2,1,0:T(8,128)S(1)}, u32[]{:S(2)}, u32[]{:S(2)}) %all-to-all-start.1) | async-done | bytes 131104 | tf_op jit(solution)/shard_map/all_to_all | solution.py:93
  78.8 5.7 %all-to-all-start.2 = ((f32[16,8,256]{2,1,0:T(8,128)}), f32[16,8,256]{2,1,0:T(8,128)S(1)}, u32[]{:S(2)}, u32[]{:S(2)}) async-start(f32[16,8,256]{2,1,0:T(8,128)} %tile.4), calls=%async_computation.2 | async-start | bytes 262144 | tf_op jit(solution)/shard_map/all_to_all | solution.py:93
  84.6 0.7 constant_dynamic-slice_fusion.2
  85.2 4.1 %collective-permute-start.2 = (f32[4,1,32,256]{3,2,1,0:T(8,128)}, f32[4,1,32,256]{3,2,1,0:T(8,128)}, u32[]{:S(2)}, u32[]{:S(2)}) collective-permute-start(f32[4,1,32,256]{3,2,1,0:T(8,128)} %constant_dynamic-slice_fusion.2), channel_id=1, source_target_pairs={{0,4},{2,6},{4,0},{6,2},{8,12},{10,14},{12,8},{14,10},{16,20},{18,... | collective-permute-start | bytes 393224 | tf_op jit(solution)/shard_map/ppermute | solution.py:116
  89.4 10.9 %collective-permute-done.2 = f32[4,1,32,256]{3,2,1,0:T(8,128)} collective-permute-done((f32[4,1,32,256]{3,2,1,0:T(8,128)}, f32[4,1,32,256]{3,2,1,0:T(8,128)}, u32[]{:S(2)}, u32[]{:S(2)}) %collective-permute-start.2) | collective-permute-done | bytes 131104 | tf_op jit(solution)/shard_map/ppermute | solution.py:116
  100.2 1.6 dynamic-slice_add_fusion.2
  101.8 1.5 tile.5
  103.3 5.8 %all-to-all-start.3 = ((f32[16,128,256]{2,1,0:T(8,128)}), f32[16,128,256]{2,1,0:T(8,128)}, u32[]{:S(2)}, u32[]{:S(2)}) async-start(f32[16,128,256]{2,1,0:T(8,128)} %tile.5), calls=%async_computation.3 | async-start | bytes 4194304 | tf_op jit(solution)/shard_map/all_to_all | solution.py:93
  109.3 7.2 %collective-permute-start.3 = (f32[2,1,32,256]{3,2,1,0:T(8,128)S(1)}, f32[2,1,32,256]{3,2,1,0:T(8,128)S(1)}, u32[]{:S(2)}, u32[]{:S(2)}) collective-permute-start(f32[2,1,32,256]{3,2,1,0:T(8,128)S(1)} %constant_dynamic-slice_fusion.1), channel_id=1, source_target_pairs={{0,8},{2,10},{4,12},{6,14},{8,0},{10,2},{12,4},{14,6},{16,24},{18,... | collective-permute-start | bytes 196616 | tf_op jit(solution)/shard_map/ppermute | solution.py:116
  116.5 1.8 %convert_reduce_fusion = s32[2048]{0:T(1024)S(1)} fusion(s32[2048]{0:T(1024)S(1)} %copy-done.4), kind=kLoop, calls=%fused_computation | loop fusion | flops 12580864 | bytes 16384 | tf_op jit(solution)/shard_map/reduce_sum | solution.py:120
  118.3 2.8 %collective-permute-done.3 = f32[2,1,32,256]{3,2,1,0:T(8,128)S(1)} collective-permute-done((f32[2,1,32,256]{3,2,1,0:T(8,128)S(1)}, f32[2,1,32,256]{3,2,1,0:T(8,128)S(1)}, u32[]{:S(2)}, u32[]{:S(2)}) %collective-permute-start.3) | collective-permute-done | bytes 65568 | tf_op jit(solution)/shard_map/ppermute | solution.py:116
  121.1 9.1 %collective-permute-start.4 = (f32[1,1,32,256]{3,2,1,0:T(8,128)S(1)}, f32[1,1,32,256]{3,2,1,0:T(8,128)S(1)}, u32[]{:S(2)}, u32[]{:S(2)}) collective-permute-start(f32[1,1,32,256]{3,2,1,0:T(8,128)S(1)} %constant_dynamic-slice_fusion), channel_id=1, source_target_pairs={{0,16},{2,18},{4,20},{6,22},{8,24},{10,26},{12,28},{14,30},{16,0},... | collective-permute-start | bytes 98312 | tf_op jit(solution)/shard_map/ppermute | solution.py:116
  130.2 4.3 %collective-permute-done.4 = f32[1,1,32,256]{3,2,1,0:T(8,128)S(1)} collective-permute-done((f32[1,1,32,256]{3,2,1,0:T(8,128)S(1)}, f32[1,1,32,256]{3,2,1,0:T(8,128)S(1)}, u32[]{:S(2)}, u32[]{:S(2)}) %collective-permute-start.4) | collective-permute-done | bytes 32800 | tf_op jit(solution)/shard_map/ppermute | solution.py:116
  134.8 26.8 %shard_map.55 = f32[32,2048]{1,0:T(8,128)S(1)} custom-call(s32[2048]{0:T(1024)S(1)} %fusion.19.where_ref, f32[2048,256]{1,0:T(8,128)} %bitcast.8.flow_ref, f32[32,256]{1,0:T(8,128)S(1)} %add_bitcast_fusion.base_ref, bf16[32,2048]{1,0:T(8,128)(2,1)S(1)} %copy-done.1, f32[32,1]{1,0:T(8,128)S(1)} %copy.9.gain_ref), custom_call_target="tpu_custom_call" | custom-call | flops 83886080 | bytes 2490368 | tf_op jit(solution)/shard_map/pallas_call | solution.py:63
  161.6 7.0 %collective-permute-start.5 = (f32[32,2048]{1,0:T(8,128)S(1)}, f32[32,2048]{1,0:T(8,128)S(1)}, u32[]{:S(2)}, u32[]{:S(2)}) collective-permute-start(f32[32,2048]{1,0:T(8,128)S(1)} %shard_map.55), channel_id=1, source_target_pairs={{0,1},{1,0},{2,3},{3,2},{4,5},{5,4},{6,7},{7,6},{8,9},{9,8},{10,11... | collective-permute-start | bytes 786440 | tf_op jit(solution)/shard_map/ppermute | solution.py:182
  168.7 1.1 collective-permute-done.5
  169.8 0.7 multiply_add_fusion
  (36 shorter events, 3.0 us)
Async XLA Ops:
  0.0 5.0 %copy-start = (bf16[1024,1536]{1,0:T(8,128)(2,1)S(1)}, bf16[1024,1536]{1,0:T(8,128)(2,1)}, u32[]{:S(2)}) copy-start(bf16[1024,1536]{1,0:T(8,128)(2,1)} %param.5) | copy-start | bytes 9437188
  11.3 34.7 %all-to-all-start = ((f32[16,64,256]{2,1,0:T(8,128)}), f32[16,64,256]{2,1,0:T(8,128)}, u32[]{:S(2)}, u32[]{:S(2)}) async-start(f32[16,64,256]{2,1,0:T(8,128)} %bitcast.23), calls=%async_computation | async-start | bytes 2097152 | tf_op jit(solution)/shard_map/all_to_all | solution.py:93
  20.9 23.2 %collective-permute-start = (f32[1,1,512,256]{3,2,1,0:T(8,128)}, f32[1,1,512,256]{3,2,1,0:T(8,128)}, u32[]{:S(2)}, u32[]{:S(2)}) collective-permute-start(f32[1,1,512,256]{3,2,1,0:T(8,128)} %constant_dynamic-slice_fusion.4), channel_id=1, source_target_pairs={{0,32},{32,0},{1,33},{33,1},{2,34},{34,2},{3,35},{35,3},{4,36},{36... | collective-permute-start | bytes 1572872 | tf_op jit(solution)/shard_map/ppermute | solution.py:116
  47.5 1.1 copy-start.2
  48.6 17.5 %collective-permute-start.1 = (f32[8,1,32,256]{3,2,1,0:T(8,128)S(1)}, f32[8,1,32,256]{3,2,1,0:T(8,128)}, u32[]{:S(2)}, u32[]{:S(2)}) collective-permute-start(f32[8,1,32,256]{3,2,1,0:T(8,128)S(1)} %constant_dynamic-slice_fusion.3), channel_id=1, source_target_pairs={{0,2},{2,0},{4,6},{6,4},{8,10},{10,8},{12,14},{14,12},{16,18},{18,... | collective-permute-start | bytes 786440 | tf_op jit(solution)/shard_map/ppermute | solution.py:116
  52.1 26.0 %all-to-all-start.1 = ((f32[16,8,256]{2,1,0:T(8,128)}), f32[16,8,256]{2,1,0:T(8,128)S(1)}, u32[]{:S(2)}, u32[]{:S(2)}) async-start(f32[16,8,256]{2,1,0:T(8,128)} %bitcast.4), calls=%async_computation.1 | async-start | bytes 262144 | tf_op jit(solution)/shard_map/all_to_all | solution.py:93
  78.8 22.9 %all-to-all-start.2 = ((f32[16,8,256]{2,1,0:T(8,128)}), f32[16,8,256]{2,1,0:T(8,128)S(1)}, u32[]{:S(2)}, u32[]{:S(2)}) async-start(f32[16,8,256]{2,1,0:T(8,128)} %tile.4), calls=%async_computation.2 | async-start | bytes 262144 | tf_op jit(solution)/shard_map/all_to_all | solution.py:93
  85.2 15.0 %collective-permute-start.2 = (f32[4,1,32,256]{3,2,1,0:T(8,128)}, f32[4,1,32,256]{3,2,1,0:T(8,128)}, u32[]{:S(2)}, u32[]{:S(2)}) collective-permute-start(f32[4,1,32,256]{3,2,1,0:T(8,128)} %constant_dynamic-slice_fusion.2), channel_id=1, source_target_pairs={{0,4},{2,6},{4,0},{6,2},{8,12},{10,14},{12,8},{14,10},{16,20},{18,... | collective-permute-start | bytes 393224 | tf_op jit(solution)/shard_map/ppermute | solution.py:116
  101.8 7.4 %copy-start.5 = (f32[32]{0:T(128)S(1)}, f32[32]{0:T(128)}, u32[]{:S(2)}) copy-start(f32[32]{0:T(128)} %param.8) | copy-start | bytes 388
  101.8 14.7 %copy-start.4 = (s32[2048]{0:T(1024)S(1)}, s32[2048]{0:T(1024)}, u32[]{:S(2)}) copy-start(s32[2048]{0:T(1024)} %param.9) | copy-start | bytes 24580
  101.8 33.0 %copy-start.1 = (bf16[32,2048]{1,0:T(8,128)(2,1)S(1)}, bf16[32,2048]{1,0:T(8,128)(2,1)}, u32[]{:S(2)}) copy-start(bf16[32,2048]{1,0:T(8,128)(2,1)} %lodf_ref.1) | copy-start | bytes 393220
  103.3 5.9 %copy-start.3 = (f32[4,1,32,256]{3,2,1,0:T(8,128)S(1)}, f32[4,1,32,256]{3,2,1,0:T(8,128)}, u32[]{:S(2)}) copy-start(f32[4,1,32,256]{3,2,1,0:T(8,128)} %dynamic-slice_add_fusion.2) | copy-start | bytes 393220
  103.3 31.5 %all-to-all-start.3 = ((f32[16,128,256]{2,1,0:T(8,128)}), f32[16,128,256]{2,1,0:T(8,128)}, u32[]{:S(2)}, u32[]{:S(2)}) async-start(f32[16,128,256]{2,1,0:T(8,128)} %tile.5), calls=%async_computation.3 | async-start | bytes 4194304 | tf_op jit(solution)/shard_map/all_to_all | solution.py:93
  109.3 11.8 %collective-permute-start.3 = (f32[2,1,32,256]{3,2,1,0:T(8,128)S(1)}, f32[2,1,32,256]{3,2,1,0:T(8,128)S(1)}, u32[]{:S(2)}, u32[]{:S(2)}) collective-permute-start(f32[2,1,32,256]{3,2,1,0:T(8,128)S(1)} %constant_dynamic-slice_fusion.1), channel_id=1, source_target_pairs={{0,8},{2,10},{4,12},{6,14},{8,0},{10,2},{12,4},{14,6},{16,24},{18,... | collective-permute-start | bytes 196616 | tf_op jit(solution)/shard_map/ppermute | solution.py:116
  121.1 13.4 %collective-permute-start.4 = (f32[1,1,32,256]{3,2,1,0:T(8,128)S(1)}, f32[1,1,32,256]{3,2,1,0:T(8,128)S(1)}, u32[]{:S(2)}, u32[]{:S(2)}) collective-permute-start(f32[1,1,32,256]{3,2,1,0:T(8,128)S(1)} %constant_dynamic-slice_fusion), channel_id=1, source_target_pairs={{0,16},{2,18},{4,20},{6,22},{8,24},{10,26},{12,28},{14,30},{16,0},... | collective-permute-start | bytes 98312 | tf_op jit(solution)/shard_map/ppermute | solution.py:116
  161.6 8.2 %collective-permute-start.5 = (f32[32,2048]{1,0:T(8,128)S(1)}, f32[32,2048]{1,0:T(8,128)S(1)}, u32[]{:S(2)}, u32[]{:S(2)}) collective-permute-start(f32[32,2048]{1,0:T(8,128)S(1)} %shard_map.55), channel_id=1, source_target_pairs={{0,1},{1,0},{2,3},{3,2},{4,5},{5,4},{6,7},{7,6},{8,9},{9,8},{10,11... | collective-permute-start | bytes 786440 | tf_op jit(solution)/shard_map/ppermute | solution.py:182
